TPU v7x, 32 devices: a whole 2x2x4 slice. The times are simulated.
32 devices in a mesh: dp: 4 (over z), seq: 8 (over y, x, core).
Axes of the slice: x: 2, y: 2, z: 4, core: 2. Of those that a mesh axis runs over, the one named last changes fastest.
Arguments:
- grad_out: bfloat16 [512, 16, 2048], P('seq', 'dp'), may hold values from -12 to 12
- query_in: bfloat16 [512, 16, 2048], P('seq', 'dp'), may hold values from -26 to 26
- rotated_key_input: bfloat16 [512, 16, 512], P('seq', 'dp'), may hold values from -6 to 6
- value_input_columns: bfloat16 [512, 16, 512], P('seq', 'dp'), may hold values from -6 to 6
- out_weight: bfloat16 [2048, 2048], P(None, 'dp'), may hold values from -0.125 to 0.125
- doc_ids: int32 [16, 512], P('dp', 'seq'), may hold values from 0 to 7, never falling along the last dimension, each value on 1 to 128 neighbouring positions
Outputs:
- query_grad: bfloat16 [512, 16, 2048], P('seq', 'dp')
- key_gradient_out: bfloat16 [512, 16, 512], P('seq', 'dp')
- value_gradient_out: bfloat16 [512, 16, 512], P('seq', 'dp')
Inputs may be any that keep to these rules, and one draw needn't show every extreme that they name: `doc_ids`: along each sequence the ids never decrease, and every document spans at most 128 positions; in each sequence some document spans exactly 128.
All inputs are finite; a program needn't handle non-finite values.
Results may differ from a plain program's by a relative error of at most 0.04.
Values may be sent and summed in bfloat16 or wider, within the bound.
A program may use at most 128 MiB of HBM per device.

v0:
```python
import math

import jax
import jax.numpy as jnp
from jax import lax
from jax.sharding import PartitionSpec as P

QUERY_HEADS = 16
KEY_VALUE_HEADS = 4
HEAD_SIZE = 128
MAXDOC = 128


def head_grads(query_heads, key_row_block, value_row_block, grad_heads, doc_row):
    length, heads_here, head_dim = query_heads.shape
    scale_factor = 1.0 / math.sqrt(head_dim)
    row_block = math.gcd(length, 256)
    window = row_block + MAXDOC
    key_form = "whd"
    pad_shape = (MAXDOC,) + key_row_block.shape[1:]
    key_padded = jnp.concatenate([jnp.zeros(pad_shape, key_row_block.dtype), key_row_block], 0)
    value_padded = jnp.concatenate(
        [jnp.zeros(pad_shape, value_row_block.dtype), value_row_block], 0
    )
    doc_padded = jnp.concatenate([jnp.full((MAXDOC,), -1, jnp.int32), doc_row], 0)
    key_acc = jnp.zeros((length + MAXDOC, heads_here, head_dim), jnp.float32)
    value_acc = jnp.zeros((length + MAXDOC, heads_here, head_dim), jnp.float32)
    query_parts = []
    for block_no in range(length // row_block):
        row_start = block_no * row_block
        query_block = query_heads[row_start : row_start + row_block]
        grad_block = grad_heads[row_start : row_start + row_block]
        key_block = key_padded[row_start : row_start + window]
        value_block = value_padded[row_start : row_start + window]
        query_pos = row_start + jnp.arange(row_block)
        key_pos = row_start - MAXDOC + jnp.arange(window)
        allowed = (key_pos[None, :] <= query_pos[:, None]) & (
            doc_padded[row_start : row_start + window][None, :]
            == doc_row[row_start : row_start + row_block][:, None]
        )
        scores = (
            jnp.einsum(
                "rhd," + key_form + "->hrw",
                query_block,
                key_block,
                preferred_element_type=jnp.float32,
            )
            * scale_factor
        )
        masked = jnp.where(allowed[None], scores, -jnp.inf)
        row_max = jnp.max(masked, axis=2, keepdims=True)
        raw_weights = jnp.exp(masked - row_max)
        weights_soft = raw_weights / jnp.sum(raw_weights, axis=2, keepdims=True)
        probs_low = weights_soft.astype(jnp.bfloat16)
        attn_out = jnp.einsum(
            "hrw," + key_form + "->rhd", probs_low, value_block, preferred_element_type=jnp.float32
        ).astype(jnp.bfloat16)
        delta_rows = jnp.sum(grad_block.astype(jnp.float32) * attn_out.astype(jnp.float32), axis=2)
        value_acc = value_acc.at[row_start : row_start + window].add(
            jnp.einsum("hrw,rhd->whd", probs_low, grad_block, preferred_element_type=jnp.float32)
        )
        grad_probs = jnp.einsum(
            "rhd," + key_form + "->hrw", grad_block, value_block, preferred_element_type=jnp.float32
        )
        grad_low = (weights_soft * (grad_probs - jnp.transpose(delta_rows)[:, :, None])).astype(
            jnp.bfloat16
        )
        query_parts.append(
            (
                jnp.einsum(
                    "hrw," + key_form + "->rhd",
                    grad_low,
                    key_block,
                    preferred_element_type=jnp.float32,
                )
                * scale_factor
            ).astype(jnp.bfloat16)
        )
        key_acc = key_acc.at[row_start : row_start + window].add(
            jnp.einsum("hrw,rhd->whd", grad_low, query_block, preferred_element_type=jnp.float32)
        )
    query_grad = jnp.concatenate(query_parts, 0)
    per_head_key_gradient = key_acc[MAXDOC:] * scale_factor
    per_head_value_gradient = value_acc[MAXDOC:]
    return (query_grad, per_head_key_gradient, per_head_value_gradient)


def body(grad_out, query_in, rotated_key_input, value_input_columns, out_weight, doc_ids):
    seq_count = lax.axis_size("seq")
    seq_index = lax.axis_index("seq")
    position_index, local_sequence_count, context_width = query_in.shape
    heads_per_group = QUERY_HEADS // KEY_VALUE_HEADS
    items_here = local_sequence_count * QUERY_HEADS // seq_count
    flat_grad = grad_out.reshape(position_index * local_sequence_count, grad_out.shape[2])
    rows_each = context_width // seq_count
    own_rows = lax.dynamic_slice_in_dim(out_weight, seq_index * rows_each, rows_each, 0)
    row_slab = lax.all_gather(own_rows, "dp", axis=1, tiled=True)
    d_context = lax.dot_general(
        flat_grad,
        lax.all_gather(row_slab, "seq", axis=0, tiled=True),
        (((1,), (1,)), ((), ())),
        preferred_element_type=jnp.float32,
    )
    d_low = d_context.astype(jnp.bfloat16)
    all_docs = lax.all_gather(doc_ids, "seq", axis=1, tiled=True)
    grad_items = d_low.reshape(position_index, local_sequence_count * QUERY_HEADS, HEAD_SIZE)
    query_items = query_in.reshape(position_index, local_sequence_count * QUERY_HEADS, HEAD_SIZE)
    own_seq = seq_index * items_here // QUERY_HEADS
    doc_row = lax.dynamic_index_in_dim(all_docs, own_seq, 0, keepdims=False)
    grad_heads = lax.all_to_all(grad_items, "seq", split_axis=1, concat_axis=0, tiled=True)
    widened_head_shape = (
        position_index,
        local_sequence_count,
        KEY_VALUE_HEADS,
        heads_per_group,
        HEAD_SIZE,
    )
    key_items = jnp.broadcast_to(
        rotated_key_input.reshape(
            position_index, local_sequence_count, KEY_VALUE_HEADS, 1, HEAD_SIZE
        ),
        widened_head_shape,
    ).reshape(position_index, local_sequence_count * QUERY_HEADS, HEAD_SIZE)
    value_items = jnp.broadcast_to(
        value_input_columns.reshape(
            position_index, local_sequence_count, KEY_VALUE_HEADS, 1, HEAD_SIZE
        ),
        widened_head_shape,
    ).reshape(position_index, local_sequence_count * QUERY_HEADS, HEAD_SIZE)
    query_heads, key_head_count, value_head_count = (
        lax.all_to_all(query_items, "seq", split_axis=1, concat_axis=0, tiled=True),
        lax.all_to_all(key_items, "seq", split_axis=1, concat_axis=0, tiled=True),
        lax.all_to_all(value_items, "seq", split_axis=1, concat_axis=0, tiled=True),
    )
    dq_parts, dk_parts, dv_parts = ([], [], [])
    for item_no in range(items_here):
        item_cols = slice(item_no, item_no + 1)
        results = head_grads(
            query_heads[:, item_cols],
            key_head_count[:, item_cols],
            value_head_count[:, item_cols],
            grad_heads[:, item_cols],
            doc_row,
        )
        dq_parts.append(results[0])
        dk_parts.append(results[1])
        dv_parts.append(results[2])
    query_back_rows = lax.all_to_all(
        jnp.concatenate(dq_parts, 1), "seq", split_axis=0, concat_axis=1, tiled=True
    )
    key_gradient_terms, value_gradient_terms = (
        lax.all_to_all(
            jnp.concatenate(dk_parts, 1), "seq", split_axis=0, concat_axis=1, tiled=True
        ),
        lax.all_to_all(
            jnp.concatenate(dv_parts, 1), "seq", split_axis=0, concat_axis=1, tiled=True
        ),
    )
    query_grad = query_back_rows.reshape(position_index, local_sequence_count, context_width)
    key_gradient_out = (
        jnp.sum(
            key_gradient_terms.reshape(
                position_index, local_sequence_count, KEY_VALUE_HEADS, heads_per_group, HEAD_SIZE
            ),
            axis=3,
        )
        .astype(jnp.bfloat16)
        .reshape(position_index, local_sequence_count, KEY_VALUE_HEADS * HEAD_SIZE)
    )
    value_gradient_out = (
        jnp.sum(
            value_gradient_terms.reshape(
                position_index, local_sequence_count, KEY_VALUE_HEADS, heads_per_group, HEAD_SIZE
            ),
            axis=3,
        )
        .astype(jnp.bfloat16)
        .reshape(position_index, local_sequence_count, KEY_VALUE_HEADS * HEAD_SIZE)
    )
    return (query_grad, key_gradient_out, value_gradient_out)


def solution(mesh):
    in_specs = (
        P("seq", "dp", None),
        P("seq", "dp", None),
        P("seq", "dp", None),
        P("seq", "dp", None),
        P(None, "dp"),
        P("dp", "seq"),
    )
    out_specs = (P("seq", "dp", None), P("seq", "dp", None), P("seq", "dp", None))
    return jax.shard_map(body, mesh=mesh, in_specs=in_specs, out_specs=out_specs, check_vma=False)
```

profile of v0, /device:TPU:0, one launch (start us, length us, event | category | flops | bytes accessed | tf_op | source)
XLA Modules:
  0.0 362.0 jit_solution(17418439694501294764)
XLA Ops:
  7.2 1.5 copy-done
  11.9 5.2 %all-to-all-start = ((bf16[64,64,128]{2,0,1:T(8,128)(2,1)}), bf16[64,64,128]{2,0,1:T(8,128)(2,1)S(1)}, u32[]{:S(2)}, u32[]{:S(2)}) async-start(bf16[64,64,128]{2,0,1:T(8,128)(2,1)} %bitcast), calls=%async_computation | async-start | bytes 2097152 | tf_op jit(solution)/shard_map/all_to_all | solution.py:132
  17.1 23.7 %all-gather.4.cloned.1.call-done = bf16[256,2048]{1,0:T(8,128)(2,1)} async-done(((bf16[256,512]{1,0:T(8,128)(2,1)}), bf16[256,2048]{1,0:T(8,128)(2,1)}) %all-gather.4.cloned.1.call-update) | async-done | bytes 1048592 | tf_op jit(solution)/shard_map/all_gather | solution.py:97
  41.6 1.6 copy.226
  43.2 3.7 %all-to-all-start.1 = ((bf16[64,64,128]{2,0,1:T(8,128)(2,1)}), bf16[64,64,128]{2,0,1:T(8,128)(2,1)S(1)}, u32[]{:S(2)}, u32[]{:S(2)}) async-start(bf16[64,64,128]{2,0,1:T(8,128)(2,1)} %copy.226), calls=%async_computation.1 | async-start | bytes 2097152 | tf_op jit(solution)/shard_map/all_to_all | solution.py:131
  47.1 24.1 %all-to-all-done.1 = bf16[64,64,128]{2,0,1:T(8,128)(2,1)S(1)} async-done(((bf16[64,64,128]{2,0,1:T(8,128)(2,1)}), bf16[64,64,128]{2,0,1:T(8,128)(2,1)S(1)}, u32[]{:S(2)}, u32[]{:S(2)}) %all-to-all-start.1) | async-done | bytes 1048608 | tf_op jit(solution)/shard_map/all_to_all | solution.py:131
  71.2 1.3 broadcast_in_dim.31
  72.5 4.2 %all-to-all-start.3 = ((bf16[64,64,128]{2,0,1:T(8,128)(2,1)}), bf16[64,64,128]{2,0,1:T(8,128)(2,1)}, u32[]{:S(2)}, u32[]{:S(2)}) async-start(bf16[64,64,128]{2,0,1:T(8,128)(2,1)} %bitcast.21), calls=%async_computation.3 | async-start | bytes 2097152 | tf_op jit(solution)/shard_map/all_to_all | solution.py:133
  76.8 29.7 %all-gather = s32[8,64,4]{1,2,0:T(4,128)S(1)} all-gather(s32[1,64,4]{1,2,0:T(4,128)S(1)} %bitcast.1083), channel_id=1, replica_groups=mesh['dp'=4,'seq'=8] {'seq'}, dimensions={0}, use_global_device_ids=true | all-gather | bytes 9216 | tf_op jit(solution)/shard_map/all_gather | solution.py:105
  106.6 2.1 reshape.2056
  110.6 1.9 copy.236
  112.5 1.9 fusion.477
  114.9 2.5 fusion.474
  121.7 1.4 fusion.479
  123.2 2.5 fusion.476
  127.8 1.3 fusion.195
  129.9 1.3 fusion.201
  134.2 1.3 fusion.205
  136.3 1.3 fusion.203
  138.8 1.3 fusion.207
  142.9 2.5 fusion.496
  145.4 1.3 fusion.248
  146.8 1.4 fusion.249
  148.2 1.4 fusion.246
  149.6 1.4 fusion.247
  151.0 1.4 fusion.244
  152.5 1.4 fusion.245
  154.6 1.4 fusion.243
  160.0 6.7 %fusion = bf16[256,2048]{0,1:T(8,128)(2,1)} fusion(bf16[2048,2048]{1,0:T(8,128)(2,1)} %all-gather.6.cloned.1.call-done, bf16[256,2048]{1,0:T(8,128)(2,1)S(1)} %copy-done.49), kind=kOutput, calls=%fused_computation.1 | convolution fusion | flops 2148007936 | bytes 10485760 | tf_op jit(solution)/shard_map/dot_general | solution.py:98
  166.7 1.5 copy.229
  168.8 1.6 copy.230
  170.4 3.9 %all-to-all-start.2 = ((bf16[64,64,128]{2,0,1:T(8,128)(2,1)}), bf16[64,64,128]{2,0,1:T(8,128)(2,1)S(1)}, u32[]{:S(2)}, u32[]{:S(2)}) async-start(bf16[64,64,128]{2,0,1:T(8,128)(2,1)} %copy.230), calls=%async_computation.2 | async-start | bytes 2097152 | tf_op jit(solution)/shard_map/all_to_all | solution.py:110
  176.3 2.3 fusion.478
  178.6 11.1 %all-to-all-done.2 = bf16[64,64,128]{2,0,1:T(8,128)(2,1)S(1)} async-done(((bf16[64,64,128]{2,0,1:T(8,128)(2,1)}), bf16[64,64,128]{2,0,1:T(8,128)(2,1)S(1)}, u32[]{:S(2)}, u32[]{:S(2)}) %all-to-all-start.2) | async-done | bytes 1048608 | tf_op jit(solution)/shard_map/all_to_all | solution.py:110
  190.4 2.9 fusion.475
  193.4 1.3 fusion.109
  201.3 1.8 convolution_bitcast_fusion.29
  205.6 1.8 fusion.188
  207.4 1.8 convolution_bitcast_fusion.27
  211.7 1.8 fusion.186
  213.5 1.8 convolution_bitcast_fusion.25
  219.6 1.9 convolution_bitcast_fusion.23
  223.9 1.8 fusion.182
  225.7 1.9 convolution_bitcast_fusion.21
  230.9 1.8 fusion.180
  232.7 1.8 convolution_bitcast_fusion.19
  238.8 1.8 convolution_bitcast_fusion.17
  265.3 1.5 copy.284
  266.8 3.9 %all-to-all-start.4 = ((bf16[512,8,128]{2,1,0:T(8,128)(2,1)}), bf16[512,8,128]{2,1,0:T(8,128)(2,1)S(1)}, u32[]{:S(2)}, u32[]{:S(2)}) async-start(bf16[512,8,128]{2,1,0:T(8,128)(2,1)} %copy.284), calls=%async_computation.4 | async-start | bytes 2097152 | tf_op jit(solution)/shard_map/all_to_all | solution.py:148
  274.2 2.5 copy.286
  282.0 4.1 %all-to-all-done.4 = bf16[512,8,128]{2,1,0:T(8,128)(2,1)S(1)} async-done(((bf16[512,8,128]{2,1,0:T(8,128)(2,1)}), bf16[512,8,128]{2,1,0:T(8,128)(2,1)S(1)}, u32[]{:S(2)}, u32[]{:S(2)}) %all-to-all-start.4) | async-done | bytes 1048608 | tf_op jit(solution)/shard_map/all_to_all | solution.py:148
  286.1 3.6 all-to-all-start.5
  289.8 1.8 slice_dynamic-update-slice_fusion.4
  291.5 1.7 slice_dynamic-update-slice_fusion.3
  293.2 1.9 fusion.84
  295.1 1.7 slice_dynamic-update-slice_fusion.2
  298.7 2.9 copy.289
  301.6 14.7 %all-to-all-done.5 = f32[512,8,128]{2,1,0:T(8,128)S(1)} async-done(((f32[512,8,128]{2,1,0:T(8,128)}), f32[512,8,128]{2,1,0:T(8,128)S(1)}, u32[]{:S(2)}, u32[]{:S(2)}) %all-to-all-start.5) | async-done | bytes 2097184 | tf_op jit(solution)/shard_map/all_to_all | solution.py:152
  316.3 1.3 copy-done.2
  317.6 4.3 %all-to-all-start.6 = ((f32[512,8,128]{2,1,0:T(8,128)}), f32[512,8,128]{2,1,0:T(8,128)}, u32[]{:S(2)}, u32[]{:S(2)}) async-start(f32[512,8,128]{2,1,0:T(8,128)} %copy.289), calls=%async_computation.6 | async-start | bytes 4194304 | tf_op jit(solution)/shard_map/all_to_all | solution.py:155
  323.4 2.0 copy.287
  326.6 22.1 %all-to-all-done.6 = f32[512,8,128]{2,1,0:T(8,128)} async-done(((f32[512,8,128]{2,1,0:T(8,128)}), f32[512,8,128]{2,1,0:T(8,128)}, u32[]{:S(2)}, u32[]{:S(2)}) %all-to-all-start.6) | async-done | bytes 2097184 | tf_op jit(solution)/shard_map/all_to_all | solution.py:155
  348.6 3.4 copy.290
  352.1 1.8 reduce_sum.339
  (607 shorter events, 91.4 us)
Async XLA Ops:
  7.2 33.6 %all-gather.4.cloned.1.call-start = ((), (), s32[]{:S(2)}) async-start(), calls=%async_computation.7 | async-start | bytes 1310720 | tf_op jit(solution)/shard_map/all_gather | solution.py:97
  10.6 30.2 %copy-start.48 = (bf16[64,4,2048]{2,1,0:T(4,128)(2,1)S(1)}, bf16[64,4,2048]{2,1,0:T(4,128)(2,1)}, u32[]{:S(2)}) copy-start(bf16[64,4,2048]{2,1,0:T(4,128)(2,1)} %param.71) | copy-start | bytes 3145732
  11.9 31.4 %all-to-all-start = ((bf16[64,64,128]{2,0,1:T(8,128)(2,1)}), bf16[64,64,128]{2,0,1:T(8,128)(2,1)S(1)}, u32[]{:S(2)}, u32[]{:S(2)}) async-start(bf16[64,64,128]{2,0,1:T(8,128)(2,1)} %bitcast), calls=%async_computation | async-start | bytes 2097152 | tf_op jit(solution)/shard_map/all_to_all | solution.py:132
  17.1 142.9 %all-gather.6.cloned.1.call-start = ((), (), s32[]{:S(2)}) async-start(), calls=%async_computation.8 | async-start | bytes 9437184 | tf_op jit(solution)/shard_map/all_gather | solution.py:100
  43.2 28.0 %all-to-all-start.1 = ((bf16[64,64,128]{2,0,1:T(8,128)(2,1)}), bf16[64,64,128]{2,0,1:T(8,128)(2,1)S(1)}, u32[]{:S(2)}, u32[]{:S(2)}) async-start(bf16[64,64,128]{2,0,1:T(8,128)(2,1)} %copy.226), calls=%async_computation.1 | async-start | bytes 2097152 | tf_op jit(solution)/shard_map/all_to_all | solution.py:131
  47.0 29.8 %copy-start.205 = (s32[4,64]{1,0:T(4,128)S(1)}, s32[4,64]{1,0:T(4,128)}, u32[]{:S(2)}) copy-start(s32[4,64]{1,0:T(4,128)} %param.75) | copy-start | bytes 3076
  71.2 37.5 %copy-start.3 = (bf16[64,64,128]{2,0,1:T(8,128)(2,1)}, bf16[64,64,128]{2,0,1:T(8,128)(2,1)S(1)}, u32[]{:S(2)}) copy-start(bf16[64,64,128]{2,0,1:T(8,128)(2,1)S(1)} %all-to-all-done.1) | copy-start | bytes 3145732
  72.5 38.1 %all-to-all-start.3 = ((bf16[64,64,128]{2,0,1:T(8,128)(2,1)}), bf16[64,64,128]{2,0,1:T(8,128)(2,1)}, u32[]{:S(2)}, u32[]{:S(2)}) async-start(bf16[64,64,128]{2,0,1:T(8,128)(2,1)} %bitcast.21), calls=%async_computation.3 | async-start | bytes 2097152 | tf_op jit(solution)/shard_map/all_to_all | solution.py:133
  114.8 12.1 %copy-start.127 = (bf16[384,1,128]{2,1,0:T(2,128)(2,1)}, bf16[384,1,128]{2,1,0:T(2,128)(2,1)S(1)}, u32[]{:S(2)}) copy-start(bf16[384,1,128]{2,1,0:T(2,128)(2,1)S(1)} %get-tuple-element.495) | copy-start | bytes 294916
  114.8 16.4 %copy-start.124 = (bf16[384,1,128]{2,1,0:T(2,128)(2,1)}, bf16[384,1,128]{2,1,0:T(2,128)(2,1)S(1)}, u32[]{:S(2)}) copy-start(bf16[384,1,128]{2,1,0:T(2,128)(2,1)S(1)} %get-tuple-element.494) | copy-start | bytes 294916
  118.7 16.7 %copy-start.126 = (bf16[384,1,128]{2,1,0:T(2,128)(2,1)}, bf16[384,1,128]{2,1,0:T(2,128)(2,1)S(1)}, u32[]{:S(2)}) copy-start(bf16[384,1,128]{2,1,0:T(2,128)(2,1)S(1)} %get-tuple-element.493) | copy-start | bytes 294916
  118.8 19.2 %copy-start.123 = (bf16[384,1,128]{2,1,0:T(2,128)(2,1)}, bf16[384,1,128]{2,1,0:T(2,128)(2,1)S(1)}, u32[]{:S(2)}) copy-start(bf16[384,1,128]{2,1,0:T(2,128)(2,1)S(1)} %get-tuple-element.492) | copy-start | bytes 294916
  120.2 20.3 %copy-start.121 = (bf16[384,1,128]{2,1,0:T(2,128)(2,1)}, bf16[384,1,128]{2,1,0:T(2,128)(2,1)S(1)}, u32[]{:S(2)}) copy-start(bf16[384,1,128]{2,1,0:T(2,128)(2,1)S(1)} %get-tuple-element.491) | copy-start | bytes 294916
  120.2 21.1 %copy-start.120 = (bf16[384,1,128]{2,1,0:T(2,128)(2,1)}, bf16[384,1,128]{2,1,0:T(2,128)(2,1)S(1)}, u32[]{:S(2)}) copy-start(bf16[384,1,128]{2,1,0:T(2,128)(2,1)S(1)} %get-tuple-element.490) | copy-start | bytes 294916
  121.7 20.4 %copy-start.119 = (bf16[384,1,128]{2,1,0:T(2,128)(2,1)}, bf16[384,1,128]{2,1,0:T(2,128)(2,1)S(1)}, u32[]{:S(2)}) copy-start(bf16[384,1,128]{2,1,0:T(2,128)(2,1)S(1)} %get-tuple-element.489) | copy-start | bytes 294916
  121.7 21.2 %copy-start.117 = (bf16[384,1,128]{2,1,0:T(2,128)(2,1)}, bf16[384,1,128]{2,1,0:T(2,128)(2,1)S(1)}, u32[]{:S(2)}) copy-start(bf16[384,1,128]{2,1,0:T(2,128)(2,1)S(1)} %get-tuple-element.488) | copy-start | bytes 294916
  123.1 14.5 %copy-start.109 = (bf16[384,1,128]{2,1,0:T(2,128)(2,1)}, bf16[384,1,128]{2,1,0:T(2,128)(2,1)S(1)}, u32[]{:S(2)}) copy-start(bf16[384,1,128]{2,1,0:T(2,128)(2,1)S(1)} %get-tuple-element.450) | copy-start | bytes 294916
  123.2 17.0 %copy-start.107 = (bf16[384,1,128]{2,1,0:T(2,128)(2,1)}, bf16[384,1,128]{2,1,0:T(2,128)(2,1)S(1)}, u32[]{:S(2)}) copy-start(bf16[384,1,128]{2,1,0:T(2,128)(2,1)S(1)} %get-tuple-element.449) | copy-start | bytes 294916
  123.2 17.7 %copy-start.105 = (bf16[384,1,128]{2,1,0:T(2,128)(2,1)}, bf16[384,1,128]{2,1,0:T(2,128)(2,1)S(1)}, u32[]{:S(2)}) copy-start(bf16[384,1,128]{2,1,0:T(2,128)(2,1)S(1)} %get-tuple-element.448) | copy-start | bytes 294916
  123.2 18.5 %copy-start.103 = (bf16[384,1,128]{2,1,0:T(2,128)(2,1)}, bf16[384,1,128]{2,1,0:T(2,128)(2,1)S(1)}, u32[]{:S(2)}) copy-start(bf16[384,1,128]{2,1,0:T(2,128)(2,1)S(1)} %get-tuple-element.447) | copy-start | bytes 294916
  123.2 19.3 %copy-start.101 = (bf16[384,1,128]{2,1,0:T(2,128)(2,1)}, bf16[384,1,128]{2,1,0:T(2,128)(2,1)S(1)}, u32[]{:S(2)}) copy-start(bf16[384,1,128]{2,1,0:T(2,128)(2,1)S(1)} %get-tuple-element.446) | copy-start | bytes 294916
  125.7 11.9 %copy-start.137 = (bf16[256,1,128]{2,1,0:T(2,128)(2,1)}, bf16[256,1,128]{2,1,0:T(2,128)(2,1)S(1)}, u32[]{:S(2)}) copy-start(bf16[256,1,128]{2,1,0:T(2,128)(2,1)S(1)} %get-tuple-element.422) | copy-start | bytes 196612
  125.8 12.3 %copy-start.148 = (bf16[256,1,128]{2,1,0:T(2,128)(2,1)}, bf16[256,1,128]{2,1,0:T(2,128)(2,1)S(1)}, u32[]{:S(2)}) copy-start(bf16[256,1,128]{2,1,0:T(2,128)(2,1)S(1)} %get-tuple-element.423) | copy-start | bytes 196612
  125.8 14.4 %copy-start.135 = (bf16[256,1,128]{2,1,0:T(2,128)(2,1)}, bf16[256,1,128]{2,1,0:T(2,128)(2,1)S(1)}, u32[]{:S(2)}) copy-start(bf16[256,1,128]{2,1,0:T(2,128)(2,1)S(1)} %get-tuple-element.420) | copy-start | bytes 196612
  125.8 14.7 %copy-start.147 = (bf16[256,1,128]{2,1,0:T(2,128)(2,1)}, bf16[256,1,128]{2,1,0:T(2,128)(2,1)S(1)}, u32[]{:S(2)}) copy-start(bf16[256,1,128]{2,1,0:T(2,128)(2,1)S(1)} %get-tuple-element.421) | copy-start | bytes 196612
  125.8 15.1 %copy-start.133 = (bf16[256,1,128]{2,1,0:T(2,128)(2,1)}, bf16[256,1,128]{2,1,0:T(2,128)(2,1)S(1)}, u32[]{:S(2)}) copy-start(bf16[256,1,128]{2,1,0:T(2,128)(2,1)S(1)} %get-tuple-element.418) | copy-start | bytes 196612
  125.8 15.5 %copy-start.146 = (bf16[256,1,128]{2,1,0:T(2,128)(2,1)}, bf16[256,1,128]{2,1,0:T(2,128)(2,1)S(1)}, u32[]{:S(2)}) copy-start(bf16[256,1,128]{2,1,0:T(2,128)(2,1)S(1)} %get-tuple-element.419) | copy-start | bytes 196612
  125.8 15.9 %copy-start.131 = (bf16[256,1,128]{2,1,0:T(2,128)(2,1)}, bf16[256,1,128]{2,1,0:T(2,128)(2,1)S(1)}, u32[]{:S(2)}) copy-start(bf16[256,1,128]{2,1,0:T(2,128)(2,1)S(1)} %get-tuple-element.416) | copy-start | bytes 196612
  125.8 16.3 %copy-start.145 = (bf16[256,1,128]{2,1,0:T(2,128)(2,1)}, bf16[256,1,128]{2,1,0:T(2,128)(2,1)S(1)}, u32[]{:S(2)}) copy-start(bf16[256,1,128]{2,1,0:T(2,128)(2,1)S(1)} %get-tuple-element.417) | copy-start | bytes 196612
  125.8 16.7 %copy-start.129 = (bf16[256,1,128]{2,1,0:T(2,128)(2,1)}, bf16[256,1,128]{2,1,0:T(2,128)(2,1)S(1)}, u32[]{:S(2)}) copy-start(bf16[256,1,128]{2,1,0:T(2,128)(2,1)S(1)} %get-tuple-element.415) | copy-start | bytes 196612
  126.1 19.3 %copy-start.20 = (f32[256,384]{0,1:T(8,128)}, f32[256,384]{0,1:T(8,128)S(1)}, u32[]{:S(2)}) copy-start(f32[256,384]{0,1:T(8,128)S(1)} %get-tuple-element.457) | copy-start | bytes 1179652
  127.8 19.0 %copy-start.44 = (f32[256,384]{0,1:T(8,128)}, f32[256,384]{0,1:T(8,128)S(1)}, u32[]{:S(2)}) copy-start(f32[256,384]{0,1:T(8,128)S(1)} %get-tuple-element.459) | copy-start | bytes 1179652
  129.9 18.2 %copy-start.26 = (f32[256,384]{0,1:T(8,128)}, f32[256,384]{0,1:T(8,128)S(1)}, u32[]{:S(2)}) copy-start(f32[256,384]{0,1:T(8,128)S(1)} %get-tuple-element.461) | copy-start | bytes 1179652
  132.1 17.5 %copy-start.42 = (f32[256,384]{0,1:T(8,128)}, f32[256,384]{0,1:T(8,128)S(1)}, u32[]{:S(2)}) copy-start(f32[256,384]{0,1:T(8,128)S(1)} %get-tuple-element.463) | copy-start | bytes 1179652
  134.2 16.8 %copy-start.28 = (f32[256,384]{0,1:T(8,128)}, f32[256,384]{0,1:T(8,128)S(1)}, u32[]{:S(2)}) copy-start(f32[256,384]{0,1:T(8,128)S(1)} %get-tuple-element.465) | copy-start | bytes 1179652
  136.3 16.1 %copy-start.40 = (f32[256,384]{0,1:T(8,128)}, f32[256,384]{0,1:T(8,128)S(1)}, u32[]{:S(2)}) copy-start(f32[256,384]{0,1:T(8,128)S(1)} %get-tuple-element.467) | copy-start | bytes 1179652
  137.9 16.0 %copy-start.22 = (f32[256,384]{0,1:T(8,128)}, f32[256,384]{0,1:T(8,128)S(1)}, u32[]{:S(2)}) copy-start(f32[256,384]{0,1:T(8,128)S(1)} %get-tuple-element.469) | copy-start | bytes 1179652
  137.9 16.0 %copy-start.181 = (f32[256]{0:T(256)}, f32[256]{0:T(256)S(1)}, u32[]{:S(2)}) copy-start(f32[256]{0:T(256)S(1)} %get-tuple-element.468) | copy-start | bytes 3076
  138.0 15.9 %copy-start.189 = (f32[256]{0:T(256)}, f32[256]{0:T(256)S(1)}, u32[]{:S(2)}) copy-start(f32[256]{0:T(256)S(1)} %fusion.209) | copy-start | bytes 3076
  138.8 15.8 %copy-start.38 = (f32[256,384]{0,1:T(8,128)}, f32[256,384]{0,1:T(8,128)S(1)}, u32[]{:S(2)}) copy-start(f32[256,384]{0,1:T(8,128)S(1)} %get-tuple-element.471) | copy-start | bytes 1179652
  140.4 15.7 %copy-start.24 = (f32[256,384]{0,1:T(8,128)}, f32[256,384]{0,1:T(8,128)S(1)}, u32[]{:S(2)}) copy-start(f32[256,384]{0,1:T(8,128)S(1)} %get-tuple-element.473) | copy-start | bytes 1179652
  140.4 15.7 %copy-start.183 = (f32[256]{0:T(256)}, f32[256]{0:T(256)S(1)}, u32[]{:S(2)}) copy-start(f32[256]{0:T(256)S(1)} %get-tuple-element.472) | copy-start | bytes 3076
  140.5 15.6 %copy-start.191 = (f32[256]{0:T(256)}, f32[256]{0:T(256)S(1)}, u32[]{:S(2)}) copy-start(f32[256]{0:T(256)S(1)} %fusion.213) | copy-start | bytes 3076
  140.8 16.0 %copy-start.36 = (f32[256,384]{0,1:T(8,128)}, f32[256,384]{0,1:T(8,128)S(1)}, u32[]{:S(2)}) copy-start(f32[256,384]{0,1:T(8,128)S(1)} %get-tuple-element.475) | copy-start | bytes 1179652
  140.8 16.0 %copy-start.201 = (f32[256]{0:T(256)}, f32[256]{0:T(256)S(1)}, u32[]{:S(2)}) copy-start(f32[256]{0:T(256)S(1)} %get-tuple-element.474) | copy-start | bytes 3076
  140.9 15.9 %copy-start.202 = (f32[256]{0:T(256)}, f32[256]{0:T(256)S(1)}, u32[]{:S(2)}) copy-start(f32[256]{0:T(256)S(1)} %fusion.211) | copy-start | bytes 3076
  141.2 16.4 %copy-start.16 = (f32[256,384]{0,1:T(8,128)}, f32[256,384]{0,1:T(8,128)S(1)}, u32[]{:S(2)}) copy-start(f32[256,384]{0,1:T(8,128)S(1)} %get-tuple-element.477) | copy-start | bytes 1179652
  141.3 16.3 %copy-start.185 = (f32[256]{0:T(256)}, f32[256]{0:T(256)S(1)}, u32[]{:S(2)}) copy-start(f32[256]{0:T(256)S(1)} %fusion.217) | copy-start | bytes 3076
  141.6 16.7 %copy-start.34 = (f32[256,384]{0,1:T(8,128)}, f32[256,384]{0,1:T(8,128)S(1)}, u32[]{:S(2)}) copy-start(f32[256,384]{0,1:T(8,128)S(1)} %get-tuple-element.479) | copy-start | bytes 1179652
  141.6 16.7 %copy-start.199 = (f32[256]{0:T(256)}, f32[256]{0:T(256)S(1)}, u32[]{:S(2)}) copy-start(f32[256]{0:T(256)S(1)} %get-tuple-element.478) | copy-start | bytes 3076
  141.7 16.6 %copy-start.200 = (f32[256]{0:T(256)}, f32[256]{0:T(256)S(1)}, u32[]{:S(2)}) copy-start(f32[256]{0:T(256)S(1)} %fusion.215) | copy-start | bytes 3076
  142.0 16.4 %copy-start.18 = (f32[256,384]{0,1:T(8,128)}, f32[256,384]{0,1:T(8,128)S(1)}, u32[]{:S(2)}) copy-start(f32[256,384]{0,1:T(8,128)S(1)} %get-tuple-element.481) | copy-start | bytes 1179652
  142.1 16.3 %copy-start.187 = (f32[256]{0:T(256)}, f32[256]{0:T(256)S(1)}, u32[]{:S(2)}) copy-start(f32[256]{0:T(256)S(1)} %fusion.221) | copy-start | bytes 3076
  142.4 16.8 %copy-start.30 = (f32[256,384]{0,1:T(8,128)}, f32[256,384]{0,1:T(8,128)S(1)}, u32[]{:S(2)}) copy-start(f32[256,384]{0,1:T(8,128)S(1)} %get-tuple-element.483) | copy-start | bytes 1179652
  142.4 16.8 %copy-start.195 = (f32[256]{0:T(256)}, f32[256]{0:T(256)S(1)}, u32[]{:S(2)}) copy-start(f32[256]{0:T(256)S(1)} %get-tuple-element.482) | copy-start | bytes 3076
  142.5 16.7 %copy-start.196 = (f32[256]{0:T(256)}, f32[256]{0:T(256)S(1)}, u32[]{:S(2)}) copy-start(f32[256]{0:T(256)S(1)} %fusion.219) | copy-start | bytes 3076
  142.8 16.5 %copy-start.14 = (f32[256,384]{0,1:T(8,128)}, f32[256,384]{0,1:T(8,128)S(1)}, u32[]{:S(2)}) copy-start(f32[256,384]{0,1:T(8,128)S(1)} %get-tuple-element.485) | copy-start | bytes 1179652
  142.9 16.4 %copy-start.193 = (f32[256]{0:T(256)}, f32[256]{0:T(256)S(1)}, u32[]{:S(2)}) copy-start(f32[256]{0:T(256)S(1)} %fusion.225) | copy-start | bytes 3076
  170.4 19.3 %all-to-all-start.2 = ((bf16[64,64,128]{2,0,1:T(8,128)(2,1)}), bf16[64,64,128]{2,0,1:T(8,128)(2,1)S(1)}, u32[]{:S(2)}, u32[]{:S(2)}) async-start(bf16[64,64,128]{2,0,1:T(8,128)(2,1)} %copy.230), calls=%async_computation.2 | async-start | bytes 2097152 | tf_op jit(solution)/shard_map/all_to_all | solution.py:110
  175.6 14.8 %copy-start.203 = (f32[256]{0:T(256)}, f32[256]{0:T(256)S(1)}, u32[]{:S(2)}) copy-start(f32[256]{0:T(256)S(1)} %fusion.223) | copy-start | bytes 3076
  223.9 11.7 %copy-start.13 = (bf16[256,384]{0,1:T(8,128)(2,1)S(1)}, bf16[256,384]{0,1:T(8,128)(2,1)}, u32[]{:S(2)}) copy-start(bf16[256,384]{0,1:T(8,128)(2,1)} %fusion.235) | copy-start | bytes 589828
  266.8 19.3 %all-to-all-start.4 = ((bf16[512,8,128]{2,1,0:T(8,128)(2,1)}), bf16[512,8,128]{2,1,0:T(8,128)(2,1)S(1)}, u32[]{:S(2)}, u32[]{:S(2)}) async-start(bf16[512,8,128]{2,1,0:T(8,128)(2,1)} %copy.284), calls=%async_computation.4 | async-start | bytes 2097152 | tf_op jit(solution)/shard_map/all_to_all | solution.py:148
  286.1 30.2 %all-to-all-start.5 = ((f32[512,8,128]{2,1,0:T(8,128)}), f32[512,8,128]{2,1,0:T(8,128)S(1)}, u32[]{:S(2)}, u32[]{:S(2)}) async-start(f32[512,8,128]{2,1,0:T(8,128)} %copy.286), calls=%async_computation.5 | async-start | bytes 4194304 | tf_op jit(solution)/shard_map/all_to_all | solution.py:152
  317.6 31.0 %all-to-all-start.6 = ((f32[512,8,128]{2,1,0:T(8,128)}), f32[512,8,128]{2,1,0:T(8,128)}, u32[]{:S(2)}, u32[]{:S(2)}) async-start(f32[512,8,128]{2,1,0:T(8,128)} %copy.289), calls=%async_computation.6 | async-start | bytes 4194304 | tf_op jit(solution)/shard_map/all_to_all | solution.py:155
  (151 other events, 608.8 us)
Sparse Core Ops, SparseCore 0:
  10.2 30.6 all-gather.3
  42.7 71.9 all-gather.5
where the time goes:
time: 367 us; the launch traced here: 362 us
  waiting for transfers between devices  99.8 us (27%)
  matrix products  86.5 us (24%)
  local copies, waits for them, and re-layouts  72.4 us (20%)
  blocking collectives  29.7 us (8%)
  starting transfers between devices  28.9 us (8%)
  other arithmetic  27.1 us (7%)
  between operations  17.6 us (5%)
    all_gather x1, blocking collectives, body(): all_docs = lax.all_gather(doc_ids, 'seq', axis=1, tiled=True)  29.7 us
    all_to_all x1, waiting for transfers between devices, body(): lax.all_to_all(query_items, 'seq', split_axis=1, concat_axis=0, tiled=True)  24.1 us
    all_gather x1, waiting for transfers between devices, body(): row_slab = lax.all_gather(own_rows, 'dp', axis=1, tiled=True)  23.7 us
    all_to_all x1, waiting for transfers between devices, body(): lax.all_to_all(jnp.concatenate(dv_parts, 1), 'seq', split_axis=0, concat_...  22.1 us
    unnamed x441, local copies, waits for them, and re-layouts  20.2 us
    dot_general x16, matrix products, head_grads(): jnp.einsum('rhd,' + key_form + '->hrw', grad_block, value_block, preferre...  16 us
    dot_general x16, matrix products, head_grads(): jnp.einsum('hrw,rhd->whd', grad_low, query_block, preferred_element_type=...  15.7 us
    dot_general x16, matrix products, head_grads(): jnp.einsum('hrw,' + key_form + '->rhd', probs_low, value_block, preferred...  15.2 us
  transfers between devices with their start and end apart: 9, of which 6 were waited for; matrix products, arithmetic and copies ran while one was open for 24% of the time, Pallas kernels for 0%

commit v1 on v0

v1 whole, which is shorter than its diff:
```python
import functools
import math

import jax
import jax.numpy as jnp
from jax import lax
from jax.experimental import pallas as pl
from jax.experimental.pallas import tpu as pltpu
from jax.sharding import PartitionSpec as P

QUERY_HEADS = 16
KEY_VALUE_HEADS = 4
HEAD_SIZE = 128
MAXDOC = 128
GROUP = QUERY_HEADS // KEY_VALUE_HEADS
GROUP_WIDTH = GROUP * HEAD_SIZE
F32 = jnp.float32
BF16 = jnp.bfloat16
NT = (((1,), (1,)), ((), ()))
TN = (((0,), (0,)), ((), ()))


def attention_kernel(
    halo, grad_ref, q_ref, k_ref, v_ref, w_ref, docq_ref, dock_ref,
    dq_ref, dkh_ref, dvh_ref, dko_ref, dvo_ref, bias, probs, dctx
):
    seqs, rows, _ = q_ref.shape
    window = k_ref.shape[1]
    back = halo * rows
    scale = 1.0 / math.sqrt(HEAD_SIZE)
    me = lax.axis_index("seq")

    qpos = lax.broadcasted_iota(jnp.int32, (rows, window), 0) + back
    kpos = lax.broadcasted_iota(jnp.int32, (rows, window), 1)
    causal = (kpos <= qpos) & (kpos + me * rows >= back)
    for b in range(seqs):
        same = dock_ref[b] == docq_ref[b]
        bias[b] = jnp.where(causal & same, 0.0, -1e30).astype(F32)

    def heads(ref, b, start):
        return jnp.concatenate(
            [ref[b, :, pl.ds(pl.multiple_of(start + h * HEAD_SIZE, HEAD_SIZE), HEAD_SIZE)] for h in range(GROUP)], 0
        )

    @pl.loop(0, KEY_VALUE_HEADS)
    def _(g):
        cols = pl.ds(pl.multiple_of(g * HEAD_SIZE, HEAD_SIZE), HEAD_SIZE)

        @pl.loop(0, seqs)
        def _(b):
            s = lax.dot_general(heads(q_ref, b, g * GROUP_WIDTH), k_ref[b, :, cols], NT, preferred_element_type=F32)
            s = s.reshape(GROUP, rows, window) * scale + bias[b][None]
            e = jnp.exp(s - jnp.max(s, axis=2, keepdims=True))
            p = e / jnp.sum(e, axis=2, keepdims=True)
            probs[g * seqs + b] = p.reshape(GROUP * rows, window).astype(BF16)

    @pl.loop(0, KEY_VALUE_HEADS)
    def _(g):
        cols = pl.ds(pl.multiple_of(g * HEAD_SIZE, HEAD_SIZE), HEAD_SIZE)
        wrows = pl.ds(pl.multiple_of(g * GROUP_WIDTH, GROUP_WIDTH), GROUP_WIDTH)
        d = lax.dot_general(grad_ref[...], w_ref[wrows, :], NT, preferred_element_type=F32)
        dctx[...] = d.astype(BF16).reshape(seqs, rows, GROUP_WIDTH)

        @pl.loop(0, seqs)
        def _(b):
            q = heads(q_ref, b, g * GROUP_WIDTH)
            do = heads(dctx, b, 0)
            k = k_ref[b, :, cols]
            p_low = probs[g * seqs + b]
            dp = lax.dot_general(do, v_ref[b, :, cols], NT, preferred_element_type=F32)
            p = p_low.astype(F32)
            delta = jnp.sum(p * dp, axis=1, keepdims=True)
            ds = (p * (dp - delta)).astype(BF16)
            dq = (jnp.dot(ds, k, preferred_element_type=F32) * scale).astype(BF16)
            for h in range(GROUP):
                dst = pl.ds(pl.multiple_of(g * GROUP_WIDTH + h * HEAD_SIZE, HEAD_SIZE), HEAD_SIZE)
                dq_ref[b, :, dst] = dq[h * rows:(h + 1) * rows]
            dk = lax.dot_general(ds, q, TN, preferred_element_type=F32) * scale
            dv = lax.dot_general(p_low, do, TN, preferred_element_type=F32)
            dkh_ref[b, :, cols] = dk[:back].astype(BF16)
            dvh_ref[b, :, cols] = dv[:back].astype(BF16)
            dko_ref[b, :, cols] = dk[back:]
            dvo_ref[b, :, cols] = dv[back:]


def body(grad_out, query_in, rotated_key_input, value_input_columns, out_weight, doc_ids):
    n = lax.axis_size("seq")
    me = lax.axis_index("seq")
    rows, seqs, width = query_in.shape
    halo = -(-(MAXDOC - 1) // rows)
    window = (halo + 1) * rows
    kv_width = rotated_key_input.shape[2]
    rows_each = width // n
    own_rows = lax.dynamic_slice_in_dim(out_weight, me * rows_each, rows_each, 0)
    weight = lax.all_gather(lax.all_gather(own_rows, "dp", axis=1, tiled=True), "seq", axis=0, tiled=True)

    def swap(x):
        return jnp.transpose(x, (1, 0, 2))

    q, grad = swap(query_in), swap(grad_out).reshape(seqs * rows, grad_out.shape[2])
    kv = jnp.stack([swap(rotated_key_input), swap(value_input_columns)])
    docs = doc_ids + 1

    def shift(x, by):
        return lax.ppermute(x, "seq", [(i, (i + by) % n) for i in range(n)])

    steps = range(halo, 0, -1)
    kv_all = jnp.concatenate([shift(kv, s) for s in steps] + [kv], 2)
    docs_all = jnp.concatenate([shift(docs, s) for s in steps] + [docs], 1)
    shapes = (
        jax.ShapeDtypeStruct((seqs, rows, width), BF16),
        jax.ShapeDtypeStruct((seqs, halo * rows, kv_width), BF16),
        jax.ShapeDtypeStruct((seqs, halo * rows, kv_width), BF16),
        jax.ShapeDtypeStruct((seqs, rows, kv_width), F32),
        jax.ShapeDtypeStruct((seqs, rows, kv_width), F32),
    )
    dq, dkh, dvh, dko, dvo = pl.pallas_call(
        functools.partial(attention_kernel, halo),
        out_shape=shapes,
        in_specs=[pl.BlockSpec(memory_space=pltpu.VMEM)] * 7,
        out_specs=[pl.BlockSpec(memory_space=pltpu.VMEM)] * 5,
        scratch_shapes=[
            pltpu.VMEM((seqs, rows, window), F32),
            pltpu.VMEM((KEY_VALUE_HEADS * seqs, GROUP * rows, window), BF16),
            pltpu.VMEM((seqs, rows, GROUP_WIDTH), BF16),
        ],
        compiler_params=pltpu.CompilerParams(vmem_limit_bytes=48 << 20),
    )(grad, q, kv_all[0], kv_all[1], weight, docs[:, :, None], docs_all[:, None, :])
    terms = jnp.stack([dkh, dvh])
    total = jnp.stack([dko, dvo])
    for j, s in enumerate(steps):
        total = total + shift(terms[:, :, j * rows:(j + 1) * rows], -s).astype(F32)
    total = total.astype(BF16)
    return swap(dq), swap(total[0]), swap(total[1])


def solution(mesh):
    in_specs = (
        P("seq", "dp", None),
        P("seq", "dp", None),
        P("seq", "dp", None),
        P("seq", "dp", None),
        P(None, "dp"),
        P("dp", "seq"),
    )
    out_specs = (P("seq", "dp", None), P("seq", "dp", None), P("seq", "dp", None))
    return jax.shard_map(body, mesh=mesh, in_specs=in_specs, out_specs=out_specs, check_vma=False)
```

time: 367 us -> 157 us (0.43)
  the two profiles are of different devices: /device:TPU:0 before, /device:TPU:1 now
where the time goes in v1:
time: 157 us; the launch traced here: 156 us
  waiting for transfers between devices  97.2 us (62%)
  Pallas kernels  21.7 us (14%)
  local copies, waits for them, and re-layouts  14.2 us (9%)
  between operations  14.2 us (9%)
  starting transfers between devices  6.42 us (4%)
  other arithmetic  2.66 us (2%)
    ppermute x6, waiting for transfers between devices, shift(): return lax.ppermute(x, 'seq', [(i, (i + by) % n) for i in range(n)])  40.2 us
    all_gather x1, waiting for transfers between devices, body(): lax.all_gather(own_rows, 'dp', axis=1, tiled=True)  30.5 us
    all_gather x1, waiting for transfers between devices, body(): lax.all_gather(lax.all_gather(own_rows, 'dp', axis=1, tiled=True), 'seq',...  26.4 us
    pallas_call x1, Pallas kernels, body(): pl.pallas_call(functools.partial(attention_kernel, halo), out_shape=shape...  21.7 us
    unnamed x18, local copies, waits for them, and re-layouts  8.96 us
    ppermute x6, starting transfers between devices, shift(): return lax.ppermute(x, 'seq', [(i, (i + by) % n) for i in range(n)])  6.34 us
  transfers between devices with their start and end apart: 8, of which 6 were waited for; matrix products, arithmetic and copies ran while one was open for 6% of the time, Pallas kernels for 0%

profile of v1, /device:TPU:1, one launch (start us, length us, event | category | flops | bytes accessed | tf_op | source)
XLA Modules:
  0.0 156.3 jit_solution(15953022973642737066)
XLA Ops:
  7.2 0.0 copy-start
  7.2 0.0 copy-start.6
  7.2 0.0 all-gather.3.cloned.1.call-start
  7.2 1.5 copy-done
  8.8 0.7 constant_dynamic-slice_fusion
  9.5 0.0 all-gather.3.cloned.1.call-update
  9.5 0.0 all-gather.5.cloned.1.call-start
  9.6 30.5 %all-gather.3.cloned.1.call-done = bf16[256,2048]{1,0:T(8,128)(2,1)} async-done(((bf16[256,512]{1,0:T(8,128)(2,1)}), bf16[256,2048]{1,0:T(8,128)(2,1)}) %all-gather.3.cloned.1.call-update) | async-done | bytes 1048592 | tf_op jit(solution)/shard_map/all_gather | solution.py:95
  40.1 0.0 all-gather.5.cloned.1.call-update
  40.1 1.1 copy_bitcast_fusion.1
  41.2 0.0 copy-start.3
  41.2 0.9 pad_maximum_fusion.1
  42.1 1.9 %collective-permute-start.1 = (bf16[2,4,64,512]{3,2,1,0:T(8,128)(2,1)}, bf16[2,4,64,512]{3,2,1,0:T(8,128)(2,1)}, u32[]{:S(2)}, u32[]{:S(2)}) collective-permute-start(bf16[2,4,64,512]{3,2,1,0:T(8,128)(2,1)} %pad_maximum_fusion.1), channel_id=1, source_target_pairs={{0,1},{1,2},{2,3},{3,4},{4,5},{5,6},{6,7},{7,0},{8,9},{9,10},{10,1... | collective-permute-start | bytes 1572872 | tf_op jit(solution)/shard_map/ppermute | solution.py:105
  44.0 1.2 collective-permute-start
  45.2 0.0 copy-done.6
  45.2 0.3 collective-permute-start.3
  45.5 1.2 collective-permute-start.2
  46.7 0.1 copy.13.docq_ref
  46.8 0.0 copy-done.3
  46.8 0.0 copy-start.5
  46.8 0.0 copy-start.4
  46.9 1.9 %copy.9 = bf16[4,64,2048]{2,1,0:T(8,128)(2,1)S(1)} copy(bf16[4,64,2048]{2,0,1:T(4,128)(2,1)} %bitcast.39) | data formatting | bytes 2097152 | tf_op jit(solution)/shard_map/transpose | solution.py:98
  48.8 0.0 copy-done.5
  48.8 1.5 copy.20
  50.3 22.6 %collective-permute-done.3 = s32[4,64]{1,0:T(4,128)S(1)} collective-permute-done((s32[4,64]{1,0:T(4,128)S(1)}, s32[4,64]{1,0:T(4,128)S(1)}, u32[]{:S(2)}, u32[]{:S(2)}) %collective-permute-start.3) | collective-permute-done | bytes 1056 | tf_op jit(solution)/shard_map/ppermute | solution.py:105
  72.9 1.8 %collective-permute-done.2 = s32[4,64]{1,0:T(4,128)S(1)} collective-permute-done((s32[4,64]{1,0:T(4,128)S(1)}, s32[4,64]{1,0:T(4,128)S(1)}, u32[]{:S(2)}, u32[]{:S(2)}) %collective-permute-start.2) | collective-permute-done | bytes 1056 | tf_op jit(solution)/shard_map/ppermute | solution.py:105
  74.8 0.1 pad_add_fusion
  74.9 0.0 collective-permute-done.1
  74.9 0.0 collective-permute-done
  74.9 0.0 copy-done.4
  74.9 1.4 maximum_maximum_fusion
  76.2 1.3 slice_bitcast_fusion
  77.6 26.4 %all-gather.5.cloned.1.call-done.w_ref = bf16[2048,2048]{1,0:T(8,128)(2,1)} async-done(((bf16[256,2048]{1,0:T(8,128)(2,1)}), bf16[2048,2048]{1,0:T(8,128)(2,1)}) %all-gather.5.cloned.1.call-update) | async-done | bytes 8388624 | tf_op jit(solution)/shard_map/all_gather | solution.py:95
  103.9 0.0 copy-start.1
  103.9 1.1 copy-done.1
  105.1 0.0 copy-start.2
  105.1 1.1 copy-done.2
  106.2 21.7 %shard_map.85 = (bf16[4,64,2048]{2,1,0:T(8,128)(2,1)S(1)}, bf16[4,128,512]{2,1,0:T(8,128)(2,1)S(1)}, bf16[4,128,512]{2,1,0:T(8,128)(2,1)S(1)}, f32[4,64,512]{2,1,0:T(8,128)S(1)}, f32[4,64,512]{2,1,0:T(8,128)S(1)}) custom-call(bf16[256,2048]{1,0:T(8,128)(2,1)S(1)} %bitcast.32, bf16[4,64,2048]{2,1,0:T(8,128)(2,1)} %bitcast.38, ...), custom_call_target="tpu_custom_call" | custom-call | tf_op jit(solution)/shard_map/pallas_call | solution.py:117
  127.9 0.1 fusion.2
  128.0 1.2 collective-permute-start.4
  129.2 0.5 collective-permute-start.5
  129.8 1.8 %copy.14 = bf16[64,4,2048]{2,1,0:T(4,128)(2,1)} copy(bf16[64,4,2048]{2,0,1:T(8,128)(2,1)S(1)} %bitcast.33) | data formatting | bytes 2097152
  131.5 9.8 %collective-permute-done.4 = bf16[2,4,64,512]{3,2,1,0:T(8,128)(2,1)S(1)} collective-permute-done((bf16[2,4,64,512]{3,2,1,0:T(8,128)(2,1)S(1)}, bf16[2,4,64,512]{3,2,1,0:T(8,128)(2,1)S(1)}, u32[]{:S(2)}, u32[]{:S(2)}) %collective-permute-start.4) | collective-permute-done | bytes 524320 | tf_op jit(solution)/shard_map/ppermute | solution.py:105
  141.3 6.0 %collective-permute-done.5 = bf16[2,4,64,512]{3,2,1,0:T(8,128)(2,1)S(1)} collective-permute-done((bf16[2,4,64,512]{3,2,1,0:T(8,128)(2,1)S(1)}, bf16[2,4,64,512]{3,2,1,0:T(8,128)(2,1)S(1)}, u32[]{:S(2)}, u32[]{:S(2)}) %collective-permute-start.5) | collective-permute-done | bytes 524320 | tf_op jit(solution)/shard_map/ppermute | solution.py:105
  147.3 0.3 fusion.1
  147.7 0.9 copy.16
  148.6 0.9 copy.15
  (3 shorter events, 0.0 us)
Async XLA Ops:
  7.2 1.6 %copy-start = (bf16[2048,512]{1,0:T(8,128)(2,1)S(1)}, bf16[2048,512]{1,0:T(8,128)(2,1)}, u32[]{:S(2)}) copy-start(bf16[2048,512]{1,0:T(8,128)(2,1)} %param.10) | copy-start | bytes 6291460
  7.2 38.0 %copy-start.6 = (s32[4,64]{1,0:T(4,128)S(1)}, s32[4,64]{1,0:T(4,128)}, u32[]{:S(2)}) copy-start(s32[4,64]{1,0:T(4,128)} %param.11) | copy-start | bytes 3076
  7.2 32.9 %all-gather.3.cloned.1.call-start = ((), (), s32[]{:S(2)}) async-start(), calls=%async_computation | async-start | bytes 1310720 | tf_op jit(solution)/shard_map/all_gather | solution.py:95
  9.5 94.4 %all-gather.5.cloned.1.call-start = ((), (), s32[]{:S(2)}) async-start(), calls=%async_computation.1 | async-start | bytes 9437184 | tf_op jit(solution)/shard_map/all_gather | solution.py:95
  41.2 5.6 %copy-start.3 = (bf16[1,4,64,512]{3,2,1,0:T(8,128)(2,1)}, bf16[1,4,64,512]{3,2,1,0:T(8,128)(2,1)S(1)}, u32[]{:S(2)}) copy-start(bf16[1,4,64,512]{3,2,1,0:T(8,128)(2,1)S(1)} %get-tuple-element.25) | copy-start | bytes 786436
  42.1 32.7 %collective-permute-start.1 = (bf16[2,4,64,512]{3,2,1,0:T(8,128)(2,1)}, bf16[2,4,64,512]{3,2,1,0:T(8,128)(2,1)}, u32[]{:S(2)}, u32[]{:S(2)}) collective-permute-start(bf16[2,4,64,512]{3,2,1,0:T(8,128)(2,1)} %pad_maximum_fusion.1), channel_id=1, source_target_pairs={{0,1},{1,2},{2,3},{3,4},{4,5},{5,6},{6,7},{7,0},{8,9},{9,10},{10,1... | collective-permute-start | bytes 1572872 | tf_op jit(solution)/shard_map/ppermute | solution.py:105
  44.0 30.9 %collective-permute-start = (bf16[2,4,64,512]{3,2,1,0:T(8,128)(2,1)}, bf16[2,4,64,512]{3,2,1,0:T(8,128)(2,1)}, u32[]{:S(2)}, u32[]{:S(2)}) collective-permute-start(bf16[2,4,64,512]{3,2,1,0:T(8,128)(2,1)} %pad_maximum_fusion.1), channel_id=1, source_target_pairs={{0,2},{1,3},{2,4},{3,5},{4,6},{5,7},{6,0},{7,1},{8,10},{9,11},{10,... | collective-permute-start | bytes 1572872 | tf_op jit(solution)/shard_map/ppermute | solution.py:105
  45.2 27.7 %collective-permute-start.3 = (s32[4,64]{1,0:T(4,128)S(1)}, s32[4,64]{1,0:T(4,128)S(1)}, u32[]{:S(2)}, u32[]{:S(2)}) collective-permute-start(s32[4,64]{1,0:T(4,128)S(1)} %get-tuple-element.22), channel_id=1, source_target_pairs={{0,1},{1,2},{2,3},{3,4},{4,5},{5,6},{6,7},{7,0},{8,9},{9,10},{10,1... | collective-permute-start | bytes 3080 | tf_op jit(solution)/shard_map/ppermute | solution.py:105
  45.5 29.3 %collective-permute-start.2 = (s32[4,64]{1,0:T(4,128)S(1)}, s32[4,64]{1,0:T(4,128)S(1)}, u32[]{:S(2)}, u32[]{:S(2)}) collective-permute-start(s32[4,64]{1,0:T(4,128)S(1)} %get-tuple-element.22), channel_id=1, source_target_pairs={{0,2},{1,3},{2,4},{3,5},{4,6},{5,7},{6,0},{7,1},{8,10},{9,11},{10,... | collective-permute-start | bytes 3080 | tf_op jit(solution)/shard_map/ppermute | solution.py:105
  46.8 1.9 %copy-start.5 = (bf16[64,4,2048]{2,1,0:T(4,128)(2,1)S(1)}, bf16[64,4,2048]{2,1,0:T(4,128)(2,1)}, u32[]{:S(2)}) copy-start(bf16[64,4,2048]{2,1,0:T(4,128)(2,1)} %param.7) | copy-start | bytes 3145732
  46.8 28.0 %copy-start.4 = (bf16[1,4,64,512]{3,2,1,0:T(8,128)(2,1)S(1)}, bf16[1,4,64,512]{3,2,1,0:T(8,128)(2,1)}, u32[]{:S(2)}) copy-start(bf16[1,4,64,512]{3,2,1,0:T(8,128)(2,1)} %copy-done.3) | copy-start | bytes 786436
  103.9 1.1 copy-start.1
  105.1 1.1 copy-start.2
  128.0 13.3 %collective-permute-start.4 = (bf16[2,4,64,512]{3,2,1,0:T(8,128)(2,1)S(1)}, bf16[2,4,64,512]{3,2,1,0:T(8,128)(2,1)S(1)}, u32[]{:S(2)}, u32[]{:S(2)}) collective-permute-start(bf16[2,4,64,512]{3,2,1,0:T(8,128)(2,1)S(1)} %get-tuple-element.18), channel_id=1, source_target_pairs={{0,6},{1,7},{2,0},{3,1},{4,2},{5,3},{6,4},{7,5},{8,14},{9,15},{10,... | collective-permute-start | bytes 1572872 | tf_op jit(solution)/shard_map/ppermute | solution.py:105
  129.2 18.1 %collective-permute-start.5 = (bf16[2,4,64,512]{3,2,1,0:T(8,128)(2,1)S(1)}, bf16[2,4,64,512]{3,2,1,0:T(8,128)(2,1)S(1)}, u32[]{:S(2)}, u32[]{:S(2)}) collective-permute-start(bf16[2,4,64,512]{3,2,1,0:T(8,128)(2,1)S(1)} %get-tuple-element.19), channel_id=1, source_target_pairs={{0,7},{1,0},{2,1},{3,2},{4,3},{5,4},{6,5},{7,6},{8,15},{9,8},{10,9... | collective-permute-start | bytes 1572872 | tf_op jit(solution)/shard_map/ppermute | solution.py:105
Sparse Core Ops, SparseCore 0:
  10.2 29.8 all-gather.2
  42.0 61.9 all-gather.4

commit v2 on v1

v2 whole, which is shorter than its diff:
```python
import functools
import math

import jax
import jax.numpy as jnp
from jax import lax
from jax.experimental import pallas as pl
from jax.experimental.pallas import tpu as pltpu
from jax.sharding import PartitionSpec as P

QUERY_HEADS = 16
KEY_VALUE_HEADS = 4
HEAD_SIZE = 128
MAXDOC = 128
GROUP = QUERY_HEADS // KEY_VALUE_HEADS
GROUP_WIDTH = GROUP * HEAD_SIZE
F32 = jnp.float32
BF16 = jnp.bfloat16
NT = (((1,), (1,)), ((), ()))
TN = (((0,), (0,)), ((), ()))
MESH = pl.DeviceIdType.MESH


def attention_kernel(
    n, depth, halo, chunks,
    grad_ref, q_ref, k_ref, v_ref, w_ref, docq_ref, doc_ref,
    dq_ref, dk_ref, dv_ref,
    bias, probs, dctx, weight, keys, values, docs, parts, landed, own,
    z_send, z_recv, cube_send, cube_recv, halo_send, halo_recv, back_send, back_recv,
):
    seqs, rows, _ = q_ref.shape
    sub, block = w_ref.shape[-2:]
    bits = n.bit_length() - 1
    chunk_width = n * sub
    per_group = chunks // KEY_VALUE_HEADS
    back = halo * rows
    window = back + rows
    scale = 1.0 / math.sqrt(HEAD_SIZE)
    me, layer = lax.axis_index("seq"), lax.axis_index("dp")
    own_bits = [lax.rem(lax.div(me, 1 << b), 2) for b in range(bits)]

    def flip(b):
        return me + (1 - 2 * own_bits[b]) * (1 << b)

    def shifted(by):
        return lax.rem(me + by + n, n)

    barrier = pltpu.get_barrier_semaphore()
    peers = [(lax.rem(layer + j, depth), me) for j in range(1, depth)]
    peers += [(layer, flip(b)) for b in range(bits)]
    peers += [(layer, shifted(s)) for d in range(1, halo + 1) for s in (d, -d)]
    for peer in peers:
        pl.semaphore_signal(barrier, inc=1, device_id=peer, device_id_type=MESH)
    pl.semaphore_wait(barrier, len(peers))

    def remote(src, dst, send, recv, target):
        return pltpu.make_async_remote_copy(
            src_ref=src, dst_ref=dst, send_sem=send, recv_sem=recv, device_id=target, device_id_type=MESH
        )

    mine = tuple(own_bits[b] for b in reversed(range(bits)))
    z_copies = [
        [
            remote(
                w_ref.at[(c,) + mine],
                weight.at[(c,) + mine + (depth - j,)],
                z_send.at[c, j - 1],
                z_recv.at[c, j - 1],
                (lax.rem(layer + j, depth), me),
            )
            for j in range(1, depth)
        ]
        for c in range(chunks)
    ]

    def cube(c, stage):
        high = list(range(1, bits))
        order = (high if c % 2 == 0 else high[::-1]) + [0]
        held = order[:stage]
        where = tuple(slice(None) if b in held else own_bits[b] for b in reversed(range(bits)))
        ref = weight.at[(c,) + where + (pl.ds(1, depth - 1),)]
        return remote(ref, ref, cube_send.at[c, stage], cube_recv.at[c, stage], (layer, flip(order[stage])))

    cube_copies = [[cube(c, s) for s in range(bits)] for c in range(chunks)]

    halo_copies = []
    for d in range(1, halo + 1):
        slot = halo - d
        place = pl.ds(slot * rows, rows)
        for i, (src, dst) in enumerate(
            ((k_ref, keys.at[:, place]), (v_ref, values.at[:, place]), (doc_ref, docs.at[slot]))
        ):
            halo_copies.append(
                remote(src, dst, halo_send.at[slot, i], halo_recv.at[slot, i], (layer, shifted(d)))
            )

    for copy in z_copies[0]:
        copy.start()
    for copy in halo_copies:
        copy.start()
    for c in range(1, chunks):
        for copy in z_copies[c]:
            copy.start()

    keys[:, back:] = k_ref[...]
    values[:, back:] = v_ref[...]
    docs[halo] = doc_ref[...]

    def heads(ref, b, start):
        return jnp.concatenate(
            [ref[b, :, start + h * HEAD_SIZE:start + (h + 1) * HEAD_SIZE] for h in range(GROUP)], 0
        )

    def mask():
        qpos = lax.broadcasted_iota(jnp.int32, (rows, rows), 0) + back
        kpos = lax.broadcasted_iota(jnp.int32, (rows, rows), 1)
        for j in range(halo + 1):
            causal = (kpos + j * rows <= qpos) & (kpos + (j + me) * rows >= back)
            for b in range(seqs):
                same = docs[j, b] == docq_ref[b]
                bias[b, :, j * rows:(j + 1) * rows] = jnp.where(causal & same, 0.0, -1e30).astype(F32)

    def forward(g):
        cols = slice(g * HEAD_SIZE, (g + 1) * HEAD_SIZE)

        @pl.loop(0, seqs)
        def _(b):
            s = lax.dot_general(heads(q_ref, b, g * GROUP_WIDTH), keys[b, :, cols], NT, preferred_element_type=F32)
            s = s.reshape(GROUP, rows, window) * scale + bias[b][None]
            e = jnp.exp(s - jnp.max(s, axis=2, keepdims=True))
            p = e / jnp.sum(e, axis=2, keepdims=True)
            probs[g * seqs + b] = p.reshape(GROUP * rows, window).astype(BF16)

    def project(c):
        d = None
        for j in range(depth):
            at = pl.ds(pl.multiple_of(lax.rem(layer + j, depth) * block, block), block)
            w = w_ref[c] if j == 0 else weight[(c,) + (slice(None),) * bits + (j,)]
            term = lax.dot_general(
                grad_ref[:, at], w.reshape(chunk_width, block), NT, preferred_element_type=F32
            )
            d = term if d is None else d + term
        start = (c % per_group) * chunk_width
        dctx[:, :, start:start + chunk_width] = d.astype(BF16).reshape(seqs, rows, chunk_width)

    def returned(g, j):
        return remote(
            parts.at[g, j], landed.at[g, j], back_send.at[g, j], back_recv.at[g, j], (layer, shifted(j - halo))
        )

    back_copies = [[returned(g, j) for j in range(halo)] for g in range(KEY_VALUE_HEADS)]

    def backward(g):
        cols = slice(g * HEAD_SIZE, (g + 1) * HEAD_SIZE)

        @pl.loop(0, seqs)
        def _(b):
            q = heads(q_ref, b, g * GROUP_WIDTH)
            do = heads(dctx, b, 0)
            k = keys[b, :, cols]
            p_low = probs[g * seqs + b]
            dp = lax.dot_general(do, values[b, :, cols], NT, preferred_element_type=F32)
            p = p_low.astype(F32)
            delta = jnp.sum(p * dp, axis=1, keepdims=True)
            ds = (p * (dp - delta)).astype(BF16)
            dq = (jnp.dot(ds, k, preferred_element_type=F32) * scale).astype(BF16)
            for h in range(GROUP):
                start = g * GROUP_WIDTH + h * HEAD_SIZE
                dq_ref[b, :, start:start + HEAD_SIZE] = dq[h * rows:(h + 1) * rows]
            dk = lax.dot_general(ds, q, TN, preferred_element_type=F32) * scale
            dv = lax.dot_general(p_low, do, TN, preferred_element_type=F32)
            for i, term in enumerate((dk, dv)):
                for j in range(halo):
                    parts[g, j, i, b] = term[j * rows:(j + 1) * rows].astype(BF16)
                own[g, i, b] = term[back:]

        for copy in back_copies[g]:
            copy.start()

    def finish(g):
        cols = slice(g * HEAD_SIZE, (g + 1) * HEAD_SIZE)
        for copy in back_copies[g]:
            copy.wait_recv()
        for i, out in enumerate((dk_ref, dv_ref)):
            total = own[g, i]
            for j in range(halo):
                total = total + landed[g, j, i].astype(F32)
            out[:, :, cols] = total.astype(BF16)

    for step in range(chunks + bits):
        for stage in range(bits, -1, -1):
            c = step - stage
            if not 0 <= c < chunks:
                continue
            if stage == 0:
                for copy in z_copies[c]:
                    copy.wait_recv()
            else:
                cube_copies[c][stage - 1].wait_recv()
            if stage < bits:
                cube_copies[c][stage].start()
        if step == 0:
            for copy in halo_copies:
                copy.wait_recv()
            mask()
        if step < KEY_VALUE_HEADS:
            forward(step)
        c = step - bits
        if c >= 0:
            project(c)
            if c % per_group == per_group - 1:
                backward(c // per_group)
                if c // per_group > 0:
                    finish(c // per_group - 1)
    finish(KEY_VALUE_HEADS - 1)

    for copy in halo_copies + sum(z_copies, []) + sum(cube_copies, []) + sum(back_copies, []):
        copy.wait_send()


def body(grad_out, query_in, rotated_key_input, value_input_columns, out_weight, doc_ids):
    n, depth = lax.axis_size("seq"), lax.axis_size("dp")
    rows, seqs, width = query_in.shape
    features, block = out_weight.shape
    bits = n.bit_length() - 1
    halo = -(-(MAXDOC - 1) // rows)
    window = (halo + 1) * rows
    kv_width = rotated_key_input.shape[2]
    chunks = KEY_VALUE_HEADS * max(1, min(2, features // (KEY_VALUE_HEADS * n * 16)))
    sub = features // (chunks * n)
    cube = (chunks,) + (2,) * bits

    def swap(x):
        return jnp.transpose(x, (1, 0, 2))

    q, grad = swap(query_in), swap(grad_out).reshape(seqs * rows, grad_out.shape[2])
    shapes = (
        jax.ShapeDtypeStruct((seqs, rows, width), BF16),
        jax.ShapeDtypeStruct((seqs, rows, kv_width), BF16),
        jax.ShapeDtypeStruct((seqs, rows, kv_width), BF16),
    )
    dma = pltpu.SemaphoreType.DMA
    dq, dk, dv = pl.pallas_call(
        functools.partial(attention_kernel, n, depth, halo, chunks),
        out_shape=shapes,
        in_specs=[pl.BlockSpec(memory_space=pltpu.VMEM)] * 7,
        out_specs=[pl.BlockSpec(memory_space=pltpu.VMEM)] * 3,
        scratch_shapes=[
            pltpu.VMEM((seqs, rows, window), F32),
            pltpu.VMEM((KEY_VALUE_HEADS * seqs, GROUP * rows, window), BF16),
            pltpu.VMEM((seqs, rows, GROUP_WIDTH), BF16),
            pltpu.VMEM(cube + (depth, sub, block), BF16),
            pltpu.VMEM((seqs, window, kv_width), BF16),
            pltpu.VMEM((seqs, window, kv_width), BF16),
            pltpu.VMEM((halo + 1, seqs, 1, rows), jnp.int32),
            pltpu.VMEM((KEY_VALUE_HEADS, halo, 2, seqs, rows, HEAD_SIZE), BF16),
            pltpu.VMEM((KEY_VALUE_HEADS, halo, 2, seqs, rows, HEAD_SIZE), BF16),
            pltpu.VMEM((KEY_VALUE_HEADS, 2, seqs, rows, HEAD_SIZE), F32),
            dma((chunks, depth - 1)),
            dma((chunks, depth - 1)),
            dma((chunks, bits)),
            dma((chunks, bits)),
            dma((halo, 3)),
            dma((halo, 3)),
            dma((KEY_VALUE_HEADS, halo)),
            dma((KEY_VALUE_HEADS, halo)),
        ],
        compiler_params=pltpu.CompilerParams(
            vmem_limit_bytes=48 << 20, collective_id=0, has_side_effects=True
        ),
    )(
        grad, q, swap(rotated_key_input), swap(value_input_columns),
        out_weight.reshape(cube + (sub, block)), doc_ids[:, :, None], doc_ids[:, None, :],
    )
    return swap(dq), swap(dk), swap(dv)


def solution(mesh):
    in_specs = (
        P("seq", "dp", None),
        P("seq", "dp", None),
        P("seq", "dp", None),
        P("seq", "dp", None),
        P(None, "dp"),
        P("dp", "seq"),
    )
    out_specs = (P("seq", "dp", None), P("seq", "dp", None), P("seq", "dp", None))
    return jax.shard_map(body, mesh=mesh, in_specs=in_specs, out_specs=out_specs, check_vma=False)
```

time: 157 us -> 102 us (0.65); the launches traced: 156 us -> 99.7 us
  waiting for transfers between devices: 97.2 us -> 0 us
  Pallas kernels: 21.7 us -> 91 us
  between operations: 14.2 us -> 0.69 us
  starting transfers between devices: 6.42 us -> 0 us
  local copies, waits for them, and re-layouts: 14.2 us -> 8 us
  other arithmetic: 2.66 us -> 0 us
    pallas_call x1, Pallas kernels: 21.7 us -> 91 us  [body(): pl.pallas_call(functools.partial(attention_kernel, n, depth, halo, chunks...]
    all_gather x2 -> x0, waiting for transfers between devices: 56.9 us -> none  [the longest x1 30.5 us: body(): lax.all_gather(own_rows, 'dp', axis=1, tiled=True)]
    ppermute x6 -> x0, waiting for transfers between devices: 40.2 us -> none  [shift(): return lax.ppermute(x, 'seq', [(i, (i + by) % n) for i in range(n)])]
    ppermute x6 -> x0, starting transfers between devices: 6.34 us -> none  [shift(): return lax.ppermute(x, 'seq', [(i, (i + by) % n) for i in range(n)])]
    unnamed x18 -> x8, local copies, waits for them, and re-layouts: 8.96 us -> 4.19 us
  transfers between devices with their start and end apart: 8 -> 0, of which waited for: 6 -> 0; matrix products, arithmetic and copies ran while one was open for 6% -> 0% of each run, Pallas kernels for 0% -> 0%
where the time goes in v2:
time: 102 us; the launch traced here: 99.7 us
  Pallas kernels  91 us (89%)
  local copies, waits for them, and re-layouts  8 us (8%)
    pallas_call x1, Pallas kernels, body(): pl.pallas_call(functools.partial(attention_kernel, n, depth, halo, chunks...  91 us
    unnamed x8, local copies, waits for them, and re-layouts  4.19 us
    transpose x2, local copies, waits for them, and re-layouts, swap(): return jnp.transpose(x, (1, 0, 2))  2.94 us

profile of v2, /device:TPU:1, one launch (start us, length us, event | category | flops | bytes accessed | tf_op | source)
XLA Modules:
  0.0 99.7 jit_solution(13632696797944543997)
XLA Ops:
  0.6 0.0 copy-start.1
  0.6 0.9 copy.20.docq_ref
  1.5 1.1 %copy_bitcast_fusion.1 = (bf16[4,64,512]{2,1,0:T(8,128)(2,1)S(1)}, bf16[4,64,512]{2,1,0:T(8,128)(2,1)S(1)}) fusion(bf16[64,4,512]{2,1,0:T(4,128)(2,1)} %param.9, bf16[64,4,512]{2,1,0:T(4,128)(2,1)} %param.8), kind=kLoop, calls=%fused_computation.1 | loop fusion | bytes 1048576 | tf_op jit(solution)/shard_map/transpose | solution.py:234
  2.7 0.0 copy-start
  2.7 1.8 %copy.16 = bf16[4,64,2048]{2,1,0:T(8,128)(2,1)S(1)} copy(bf16[4,64,2048]{2,0,1:T(4,128)(2,1)} %bitcast.23) | data formatting | bytes 2097152 | tf_op jit(solution)/shard_map/transpose | solution.py:234
  4.5 0.0 copy-done.1
  4.5 0.6 copy.27
  5.1 0.0 copy-done
  5.1 91.0 %shard_map.85 = (bf16[4,64,2048]{2,1,0:T(8,128)(2,1)S(1)}, bf16[4,64,512]{2,1,0:T(8,128)(2,1)S(1)}, bf16[4,64,512]{2,1,0:T(8,128)(2,1)S(1)}) custom-call(bf16[256,2048]{1,0:T(8,128)(2,1)S(1)} %bitcast.15, bf16[4,64,2048]{2,1,0:T(8,128)(2,1)S(1)} %bitcast.16, bf16[4,64,512]{2,1,0:T(8,128)(2,1)S(1)} %get-tuple-element.16.k_ref, ...), custom_call_target="tpu_custom_call" | custom-call | tf_op jit(solution)/shard_map/pallas_call | solution.py:243
  96.1 1.8 %copy.21 = bf16[64,4,2048]{2,1,0:T(4,128)(2,1)} copy(bf16[64,4,2048]{2,0,1:T(8,128)(2,1)S(1)} %bitcast.17) | data formatting | bytes 2097152
  97.9 0.9 copy.22
  98.8 0.9 copy.23
Async XLA Ops:
  0.6 3.9 %copy-start.1 = (bf16[64,4,2048]{2,1,0:T(4,128)(2,1)S(1)}, bf16[64,4,2048]{2,1,0:T(4,128)(2,1)}, u32[]{:S(2)}) copy-start(bf16[64,4,2048]{2,1,0:T(4,128)(2,1)} %param.7) | copy-start | bytes 3145732
  2.7 2.4 %copy-start = (s32[4,64]{1,0:T(4,128)S(1)}, s32[4,64]{1,0:T(4,128)}, u32[]{:S(2)}) copy-start(s32[4,64]{1,0:T(4,128)} %param.11) | copy-start | bytes 3076

commit v3 on v2

--- a/solution.py
+++ b/solution.py
@@ -48,7 +48,7 @@
     barrier = pltpu.get_barrier_semaphore()
     peers = [(lax.rem(layer + j, depth), me) for j in range(1, depth)]
     peers += [(layer, flip(b)) for b in range(bits)]
-    peers += [(layer, shifted(s)) for d in range(1, halo + 1) for s in (d, -d)]
+    peers += [(layer, shifted(s)) for s in (1, -1)]
     for peer in peers:
         pl.semaphore_signal(barrier, inc=1, device_id=peer, device_id_type=MESH)
     pl.semaphore_wait(barrier, len(peers))
@@ -75,7 +75,7 @@
 
     def cube(c, stage):
         high = list(range(1, bits))
-        order = (high if c % 2 == 0 else high[::-1]) + [0]
+        order = high + [0]
         held = order[:stage]
         where = tuple(slice(None) if b in held else own_bits[b] for b in reversed(range(bits)))
         ref = weight.at[(c,) + where + (pl.ds(1, depth - 1),)]
@@ -84,19 +84,24 @@
     cube_copies = [[cube(c, s) for s in range(bits)] for c in range(chunks)]
 
     halo_copies = []
-    for d in range(1, halo + 1):
-        slot = halo - d
-        place = pl.ds(slot * rows, rows)
-        for i, (src, dst) in enumerate(
-            ((k_ref, keys.at[:, place]), (v_ref, values.at[:, place]), (doc_ref, docs.at[slot]))
-        ):
-            halo_copies.append(
-                remote(src, dst, halo_send.at[slot, i], halo_recv.at[slot, i], (layer, shifted(d)))
-            )
+    for hop in range(halo):
+        slot = halo - 1 - hop
+        place, source = pl.ds(slot * rows, rows), pl.ds((slot + 1) * rows, rows)
+        pairs = (
+            (k_ref if hop == 0 else keys.at[:, source], keys.at[:, place]),
+            (v_ref if hop == 0 else values.at[:, source], values.at[:, place]),
+            (doc_ref if hop == 0 else docs.at[slot + 1], docs.at[slot]),
+        )
+        halo_copies.append(
+            [
+                remote(src, dst, halo_send.at[hop, i], halo_recv.at[hop, i], (layer, shifted(1)))
+                for i, (src, dst) in enumerate(pairs)
+            ]
+        )
 
     for copy in z_copies[0]:
         copy.start()
-    for copy in halo_copies:
+    for copy in halo_copies[0]:
         copy.start()
     for c in range(1, chunks):
         for copy in z_copies[c]:
@@ -145,7 +150,7 @@
 
     def returned(g, j):
         return remote(
-            parts.at[g, j], landed.at[g, j], back_send.at[g, j], back_recv.at[g, j], (layer, shifted(j - halo))
+            parts.at[g, j], landed.at[g, j], back_send.at[g, j], back_recv.at[g, j], (layer, shifted(-1))
         )
 
     back_copies = [[returned(g, j) for j in range(halo)] for g in range(KEY_VALUE_HEADS)]
@@ -174,18 +179,19 @@
                     parts[g, j, i, b] = term[j * rows:(j + 1) * rows].astype(BF16)
                 own[g, i, b] = term[back:]
 
-        for copy in back_copies[g]:
-            copy.start()
+        back_copies[g][0].start()
+
+    def relay(g):
+        for j in range(1, halo):
+            back_copies[g][j - 1].wait_recv()
+            parts[g, j] = (parts[g, j].astype(F32) + landed[g, j - 1].astype(F32)).astype(BF16)
+            back_copies[g][j].start()
 
     def finish(g):
         cols = slice(g * HEAD_SIZE, (g + 1) * HEAD_SIZE)
-        for copy in back_copies[g]:
-            copy.wait_recv()
+        back_copies[g][halo - 1].wait_recv()
         for i, out in enumerate((dk_ref, dv_ref)):
-            total = own[g, i]
-            for j in range(halo):
-                total = total + landed[g, j, i].astype(F32)
-            out[:, :, cols] = total.astype(BF16)
+            out[:, :, cols] = (own[g, i] + landed[g, halo - 1, i].astype(F32)).astype(BF16)
 
     for step in range(chunks + bits):
         for stage in range(bits, -1, -1):
@@ -199,22 +205,30 @@
                 cube_copies[c][stage - 1].wait_recv()
             if stage < bits:
                 cube_copies[c][stage].start()
-        if step == 0:
-            for copy in halo_copies:
+        if step < halo:
+            for copy in halo_copies[step]:
                 copy.wait_recv()
-            mask()
-        if step < KEY_VALUE_HEADS:
-            forward(step)
+            if step + 1 < halo:
+                for copy in halo_copies[step + 1]:
+                    copy.start()
+            else:
+                mask()
+        if 0 <= step - halo + 1 < KEY_VALUE_HEADS:
+            forward(step - halo + 1)
         c = step - bits
         if c >= 0:
             project(c)
             if c % per_group == per_group - 1:
-                backward(c // per_group)
-                if c // per_group > 0:
-                    finish(c // per_group - 1)
+                group = c // per_group
+                if group > 0:
+                    relay(group - 1)
+                backward(group)
+                if group > 0:
+                    finish(group - 1)
+    relay(KEY_VALUE_HEADS - 1)
     finish(KEY_VALUE_HEADS - 1)
 
-    for copy in halo_copies + sum(z_copies, []) + sum(cube_copies, []) + sum(back_copies, []):
+    for copy in sum(halo_copies, []) + sum(z_copies, []) + sum(cube_copies, []) + sum(back_copies, []):
         copy.wait_send()
 
 

time: 102 us -> 88.2 us (0.86); the launches traced: 99.7 us -> 88 us
  Pallas kernels: 91 us -> 79.3 us
    pallas_call x1, Pallas kernels: 91 us -> 79.3 us  [body(): pl.pallas_call(functools.partial(attention_kernel, n, depth, halo, chunks...]
where the time goes in v3:
time: 88.2 us; the launch traced here: 88 us
  Pallas kernels  79.3 us (90%)
  local copies, waits for them, and re-layouts  8 us (9%)
    pallas_call x1, Pallas kernels, body(): pl.pallas_call(functools.partial(attention_kernel, n, depth, halo, chunks...  79.3 us
    unnamed x8, local copies, waits for them, and re-layouts  4.19 us
    transpose x2, local copies, waits for them, and re-layouts, swap(): return jnp.transpose(x, (1, 0, 2))  2.94 us

profile of v3, /device:TPU:1, one launch (start us, length us, event | category | flops | bytes accessed | tf_op | source)
XLA Modules:
  0.0 88.0 jit_solution(2556818165876798324)
XLA Ops:
  0.6 0.0 copy-start.1
  0.6 0.9 copy.20.docq_ref
  1.5 1.1 %copy_bitcast_fusion.1 = (bf16[4,64,512]{2,1,0:T(8,128)(2,1)S(1)}, bf16[4,64,512]{2,1,0:T(8,128)(2,1)S(1)}) fusion(bf16[64,4,512]{2,1,0:T(4,128)(2,1)} %param.9, bf16[64,4,512]{2,1,0:T(4,128)(2,1)} %param.8), kind=kLoop, calls=%fused_computation.1 | loop fusion | bytes 1048576 | tf_op jit(solution)/shard_map/transpose | solution.py:248
  2.7 0.0 copy-start
  2.7 1.8 %copy.16 = bf16[4,64,2048]{2,1,0:T(8,128)(2,1)S(1)} copy(bf16[4,64,2048]{2,0,1:T(4,128)(2,1)} %bitcast.23) | data formatting | bytes 2097152 | tf_op jit(solution)/shard_map/transpose | solution.py:248
  4.5 0.0 copy-done.1
  4.5 0.6 copy.27
  5.1 0.0 copy-done
  5.1 79.3 %shard_map.85 = (bf16[4,64,2048]{2,1,0:T(8,128)(2,1)S(1)}, bf16[4,64,512]{2,1,0:T(8,128)(2,1)S(1)}, bf16[4,64,512]{2,1,0:T(8,128)(2,1)S(1)}) custom-call(bf16[256,2048]{1,0:T(8,128)(2,1)S(1)} %bitcast.15, bf16[4,64,2048]{2,1,0:T(8,128)(2,1)S(1)} %bitcast.16, bf16[4,64,512]{2,1,0:T(8,128)(2,1)S(1)} %get-tuple-element.16.k_ref, ...), custom_call_target="tpu_custom_call" | custom-call | tf_op jit(solution)/shard_map/pallas_call | solution.py:257
  84.4 1.8 %copy.21 = bf16[64,4,2048]{2,1,0:T(4,128)(2,1)} copy(bf16[64,4,2048]{2,0,1:T(8,128)(2,1)S(1)} %bitcast.17) | data formatting | bytes 2097152
  86.1 0.9 %copy.22 = bf16[64,4,512]{2,1,0:T(4,128)(2,1)} copy(bf16[64,4,512]{2,0,1:T(8,128)(2,1)S(1)} %bitcast.19) | data formatting | bytes 524288
  87.0 0.9 %copy.23 = bf16[64,4,512]{2,1,0:T(4,128)(2,1)} copy(bf16[64,4,512]{2,0,1:T(8,128)(2,1)S(1)} %bitcast.18) | data formatting | bytes 524288
Async XLA Ops:
  0.6 3.9 %copy-start.1 = (bf16[64,4,2048]{2,1,0:T(4,128)(2,1)S(1)}, bf16[64,4,2048]{2,1,0:T(4,128)(2,1)}, u32[]{:S(2)}) copy-start(bf16[64,4,2048]{2,1,0:T(4,128)(2,1)} %param.7) | copy-start | bytes 3145732
  2.7 2.4 %copy-start = (s32[4,64]{1,0:T(4,128)S(1)}, s32[4,64]{1,0:T(4,128)}, u32[]{:S(2)}) copy-start(s32[4,64]{1,0:T(4,128)} %param.11) | copy-start | bytes 3076

commit v4 on v3

--- a/solution.py
+++ b/solution.py
@@ -19,6 +19,7 @@
 NT = (((1,), (1,)), ((), ()))
 TN = (((0,), (0,)), ((), ()))
 MESH = pl.DeviceIdType.MESH
+LAG = 2
 
 
 def attention_kernel(
@@ -31,7 +32,6 @@
     seqs, rows, _ = q_ref.shape
     sub, block = w_ref.shape[-2:]
     bits = n.bit_length() - 1
-    chunk_width = n * sub
     per_group = chunks // KEY_VALUE_HEADS
     back = halo * rows
     window = back + rows
@@ -75,7 +75,7 @@
 
     def cube(c, stage):
         high = list(range(1, bits))
-        order = high + [0]
+        order = (high if c % 2 == 0 else high[::-1]) + [0]
         held = order[:stage]
         where = tuple(slice(None) if b in held else own_bits[b] for b in reversed(range(bits)))
         ref = weight.at[(c,) + where + (pl.ds(1, depth - 1),)]
@@ -136,17 +136,17 @@
             p = e / jnp.sum(e, axis=2, keepdims=True)
             probs[g * seqs + b] = p.reshape(GROUP * rows, window).astype(BF16)
 
-    def project(c):
+    def project(g):
         d = None
+        span = slice(g * per_group, (g + 1) * per_group)
         for j in range(depth):
             at = pl.ds(pl.multiple_of(lax.rem(layer + j, depth) * block, block), block)
-            w = w_ref[c] if j == 0 else weight[(c,) + (slice(None),) * bits + (j,)]
+            w = w_ref[span] if j == 0 else weight[(span,) + (slice(None),) * bits + (j,)]
             term = lax.dot_general(
-                grad_ref[:, at], w.reshape(chunk_width, block), NT, preferred_element_type=F32
+                grad_ref[:, at], w.reshape(GROUP_WIDTH, block), NT, preferred_element_type=F32
             )
             d = term if d is None else d + term
-        start = (c % per_group) * chunk_width
-        dctx[:, :, start:start + chunk_width] = d.astype(BF16).reshape(seqs, rows, chunk_width)
+        dctx[...] = d.astype(BF16).reshape(seqs, rows, GROUP_WIDTH)
 
     def returned(g, j):
         return remote(
@@ -193,9 +193,9 @@
         for i, out in enumerate((dk_ref, dv_ref)):
             out[:, :, cols] = (own[g, i] + landed[g, halo - 1, i].astype(F32)).astype(BF16)
 
-    for step in range(chunks + bits):
+    for step in range(chunks + LAG * bits):
         for stage in range(bits, -1, -1):
-            c = step - stage
+            c = step - LAG * stage
             if not 0 <= c < chunks:
                 continue
             if stage == 0:
@@ -215,16 +215,15 @@
                 mask()
         if 0 <= step - halo + 1 < KEY_VALUE_HEADS:
             forward(step - halo + 1)
-        c = step - bits
-        if c >= 0:
-            project(c)
-            if c % per_group == per_group - 1:
-                group = c // per_group
-                if group > 0:
-                    relay(group - 1)
-                backward(group)
-                if group > 0:
-                    finish(group - 1)
+        c = step - LAG * bits
+        if c >= 0 and c % per_group == per_group - 1:
+            group = c // per_group
+            project(group)
+            if group > 0:
+                relay(group - 1)
+            backward(group)
+            if group > 0:
+                finish(group - 1)
     relay(KEY_VALUE_HEADS - 1)
     finish(KEY_VALUE_HEADS - 1)
 

time: 88.2 us -> 74 us (0.84)
  Pallas kernels: 79.3 us -> 65.1 us
    pallas_call x1, Pallas kernels: 79.3 us -> 65.1 us  [body(): pl.pallas_call(functools.partial(attention_kernel, n, depth, halo, chunks...]
where the time goes in v4:
time: 74 us; the launch traced here: 73.8 us
  Pallas kernels  65.1 us (88%)
  local copies, waits for them, and re-layouts  8 us (11%)
    pallas_call x1, Pallas kernels, body(): pl.pallas_call(functools.partial(attention_kernel, n, depth, halo, chunks...  65.1 us
    unnamed x8, local copies, waits for them, and re-layouts  4.19 us
    transpose x2, local copies, waits for them, and re-layouts, swap(): return jnp.transpose(x, (1, 0, 2))  2.94 us

profile of v4, /device:TPU:1, one launch (start us, length us, event | category | flops | bytes accessed | tf_op | source)
XLA Modules:
  0.0 73.8 jit_solution(1814411438942659473)
XLA Ops:
  0.6 0.0 copy-start.1
  0.6 0.9 %copy.20.docq_ref = s32[4,64,1]{2,1,0:T(8,128)S(1)} copy(s32[4,64,1]{1,0,2:T(4,128)} %bitcast.20) | data formatting | bytes 2048 | tf_op jit(solution)/shard_map/broadcast_in_dim | solution.py:286
  1.5 1.1 %copy_bitcast_fusion.1 = (bf16[4,64,512]{2,1,0:T(8,128)(2,1)S(1)}, bf16[4,64,512]{2,1,0:T(8,128)(2,1)S(1)}) fusion(bf16[64,4,512]{2,1,0:T(4,128)(2,1)} %param.9, bf16[64,4,512]{2,1,0:T(4,128)(2,1)} %param.8), kind=kLoop, calls=%fused_computation.1 | loop fusion | bytes 1048576 | tf_op jit(solution)/shard_map/transpose | solution.py:247
  2.7 0.0 copy-start
  2.7 1.8 %copy.16 = bf16[4,64,2048]{2,1,0:T(8,128)(2,1)S(1)} copy(bf16[4,64,2048]{2,0,1:T(4,128)(2,1)} %bitcast.23) | data formatting | bytes 2097152 | tf_op jit(solution)/shard_map/transpose | solution.py:247
  4.5 0.0 copy-done.1
  4.5 0.6 copy.27
  5.1 0.0 copy-done
  5.1 65.1 %shard_map.85 = (bf16[4,64,2048]{2,1,0:T(8,128)(2,1)S(1)}, bf16[4,64,512]{2,1,0:T(8,128)(2,1)S(1)}, bf16[4,64,512]{2,1,0:T(8,128)(2,1)S(1)}) custom-call(bf16[256,2048]{1,0:T(8,128)(2,1)S(1)} %bitcast.15, bf16[4,64,2048]{2,1,0:T(8,128)(2,1)S(1)} %bitcast.16, bf16[4,64,512]{2,1,0:T(8,128)(2,1)S(1)} %get-tuple-element.16.k_ref, ...), custom_call_target="tpu_custom_call" | custom-call | tf_op jit(solution)/shard_map/pallas_call | solution.py:256
  70.2 1.8 %copy.21 = bf16[64,4,2048]{2,1,0:T(4,128)(2,1)} copy(bf16[64,4,2048]{2,0,1:T(8,128)(2,1)S(1)} %bitcast.17) | data formatting | bytes 2097152
  71.9 0.9 %copy.22 = bf16[64,4,512]{2,1,0:T(4,128)(2,1)} copy(bf16[64,4,512]{2,0,1:T(8,128)(2,1)S(1)} %bitcast.19) | data formatting | bytes 524288
  72.9 0.9 %copy.23 = bf16[64,4,512]{2,1,0:T(4,128)(2,1)} copy(bf16[64,4,512]{2,0,1:T(8,128)(2,1)S(1)} %bitcast.18) | data formatting | bytes 524288
Async XLA Ops:
  0.6 3.9 %copy-start.1 = (bf16[64,4,2048]{2,1,0:T(4,128)(2,1)S(1)}, bf16[64,4,2048]{2,1,0:T(4,128)(2,1)}, u32[]{:S(2)}) copy-start(bf16[64,4,2048]{2,1,0:T(4,128)(2,1)} %param.7) | copy-start | bytes 3145732
  2.7 2.4 %copy-start = (s32[4,64]{1,0:T(4,128)S(1)}, s32[4,64]{1,0:T(4,128)}, u32[]{:S(2)}) copy-start(s32[4,64]{1,0:T(4,128)} %param.11) | copy-start | bytes 3076

commit v5 on v4

--- a/solution.py
+++ b/solution.py
@@ -213,8 +213,8 @@
                     copy.start()
             else:
                 mask()
-        if 0 <= step - halo + 1 < KEY_VALUE_HEADS:
-            forward(step - halo + 1)
+        if 0 <= step - halo - 1 < KEY_VALUE_HEADS:
+            forward(step - halo - 1)
         c = step - LAG * bits
         if c >= 0 and c % per_group == per_group - 1:
             group = c // per_group

time: 74 us -> 71.7 us (0.969)
  Pallas kernels: 65.1 us -> 62.8 us
    pallas_call x1, Pallas kernels: 65.1 us -> 62.8 us  [body(): pl.pallas_call(functools.partial(attention_kernel, n, depth, halo, chunks...]
where the time goes in v5:
time: 71.7 us; the launch traced here: 71.5 us
  Pallas kernels  62.8 us (88%)
  local copies, waits for them, and re-layouts  8 us (11%)
    pallas_call x1, Pallas kernels, body(): pl.pallas_call(functools.partial(attention_kernel, n, depth, halo, chunks...  62.8 us
    unnamed x8, local copies, waits for them, and re-layouts  4.19 us
    transpose x2, local copies, waits for them, and re-layouts, swap(): return jnp.transpose(x, (1, 0, 2))  2.94 us

profile of v5, /device:TPU:1, one launch (start us, length us, event | category | flops | bytes accessed | tf_op | source)
XLA Modules:
  0.0 71.5 jit_solution(1802159132076880370)
XLA Ops:
  0.6 0.0 copy-start.1
  0.6 0.9 %copy.20.docq_ref = s32[4,64,1]{2,1,0:T(8,128)S(1)} copy(s32[4,64,1]{1,0,2:T(4,128)} %bitcast.20) | data formatting | bytes 2048 | tf_op jit(solution)/shard_map/broadcast_in_dim | solution.py:286
  1.5 1.1 %copy_bitcast_fusion.1 = (bf16[4,64,512]{2,1,0:T(8,128)(2,1)S(1)}, bf16[4,64,512]{2,1,0:T(8,128)(2,1)S(1)}) fusion(bf16[64,4,512]{2,1,0:T(4,128)(2,1)} %param.9, bf16[64,4,512]{2,1,0:T(4,128)(2,1)} %param.8), kind=kLoop, calls=%fused_computation.1 | loop fusion | bytes 1048576 | tf_op jit(solution)/shard_map/transpose | solution.py:247
  2.7 0.0 copy-start
  2.7 1.8 %copy.16 = bf16[4,64,2048]{2,1,0:T(8,128)(2,1)S(1)} copy(bf16[4,64,2048]{2,0,1:T(4,128)(2,1)} %bitcast.23) | data formatting | bytes 2097152 | tf_op jit(solution)/shard_map/transpose | solution.py:247
  4.5 0.0 copy-done.1
  4.5 0.6 copy.27
  5.1 0.0 copy-done
  5.1 62.8 %shard_map.85 = (bf16[4,64,2048]{2,1,0:T(8,128)(2,1)S(1)}, bf16[4,64,512]{2,1,0:T(8,128)(2,1)S(1)}, bf16[4,64,512]{2,1,0:T(8,128)(2,1)S(1)}) custom-call(bf16[256,2048]{1,0:T(8,128)(2,1)S(1)} %bitcast.15, bf16[4,64,2048]{2,1,0:T(8,128)(2,1)S(1)} %bitcast.16, bf16[4,64,512]{2,1,0:T(8,128)(2,1)S(1)} %get-tuple-element.16.k_ref, ...), custom_call_target="tpu_custom_call" | custom-call | tf_op jit(solution)/shard_map/pallas_call | solution.py:256
  67.9 1.8 %copy.21 = bf16[64,4,2048]{2,1,0:T(4,128)(2,1)} copy(bf16[64,4,2048]{2,0,1:T(8,128)(2,1)S(1)} %bitcast.17) | data formatting | bytes 2097152
  69.7 0.9 %copy.22 = bf16[64,4,512]{2,1,0:T(4,128)(2,1)} copy(bf16[64,4,512]{2,0,1:T(8,128)(2,1)S(1)} %bitcast.19) | data formatting | bytes 524288
  70.6 0.9 %copy.23 = bf16[64,4,512]{2,1,0:T(4,128)(2,1)} copy(bf16[64,4,512]{2,0,1:T(8,128)(2,1)S(1)} %bitcast.18) | data formatting | bytes 524288
Async XLA Ops:
  0.6 3.9 %copy-start.1 = (bf16[64,4,2048]{2,1,0:T(4,128)(2,1)S(1)}, bf16[64,4,2048]{2,1,0:T(4,128)(2,1)}, u32[]{:S(2)}) copy-start(bf16[64,4,2048]{2,1,0:T(4,128)(2,1)} %param.7) | copy-start | bytes 3145732
  2.7 2.4 %copy-start = (s32[4,64]{1,0:T(4,128)S(1)}, s32[4,64]{1,0:T(4,128)}, u32[]{:S(2)}) copy-start(s32[4,64]{1,0:T(4,128)} %param.11) | copy-start | bytes 3076
